TPU v7x, 32 devices: a whole 2x2x4 slice. The times are simulated.
32 devices in a mesh: groups: 2 (over y), seq: 4 (over z), dp: 4 (over x, core).
Axes of the slice: x: 2, y: 2, z: 4, core: 2. Of those that a mesh axis runs over, the one named last changes fastest.
Arguments:
- acceptance_gate: bfloat16 [8, 512, 1280], P(('groups', 'dp'), 'seq'), parts along dimension 0, may hold values from -6 to 6
- logarithmic_fade_factor: bfloat16 [8, 512, 1280], P(('groups', 'dp'), 'seq'), parts along dimension 0, may hold values from -12 to 0
- probe_matrix: bfloat16 [8, 512, 1280], P(('groups', 'dp'), 'seq'), parts along dimension 0, may hold values from -0.75 to 0.75
- payload_matrix: bfloat16 [8, 512, 1280], P(('groups', 'dp'), 'seq'), parts along dimension 0, may hold values from -6 to 6
- erasure_vector: bfloat16 [8, 512, 1280], P(('groups', 'dp'), 'seq'), parts along dimension 0, may hold values from -6 to 6
- inplace_update_step: bfloat16 [8, 512, 1280], P(('groups', 'dp'), 'seq'), parts along dimension 0, may hold values from 0.0079956055 to 0.019897461
- extra_probe_factor: float32 [1280], replicated, may hold values from -3 to 3
- group_scaling_factor: float32 [1280], replicated, may hold values from 0.5 to 1.5
Outputs:
- blended_signal: bfloat16 [8, 512, 1280], P(('groups', 'dp'), 'seq'), parts along dimension 0
- final_state: float32 [8, 1280, 64], P(('groups', 'dp'), 'seq'), parts along dimension 0
There are 2 independent parts, one for each index of `groups`. A program takes and returns all parts, laid end to end along the dimension named above; an argument that names none is the same for every part. Nothing has to cross between parts.
All inputs are finite; a program needn't handle non-finite values.
Results may differ from a plain program's by a relative error of at most 0.001.
Values sent between devices are 32-bit elements; how exact they have to be, the bound alone decides.
No kernel may reach another device: no remote copies, remote signals or barrier semaphores. Data moves between devices by JAX's collectives and lax.ppermute only.
A program may use at most 64 MiB of HBM per device.

v0:
```python
import jax
import jax.numpy as jnp
from jax import lax
from jax.sharding import PartitionSpec as P

GROUP_DIMENSION = 64
BLOCK = 64


HIGHEST_PRECISION = lax.Precision.HIGHEST
SCORE_PRECISION = lax.Precision.HIGH
KEY_EPS = 1e-05
NORM_EPS = 0.00064


def passed_along(shard, axis, by):
    devices = lax.axis_size(axis)
    pairs = [(i, i + by) for i in range(devices) if 0 <= i + by < devices]
    return lax.ppermute(shard, axis, pairs)


def broadcast(value, axis, source):
    kept = jnp.where(lax.axis_index(axis) == source, value, 0).astype(value.dtype)
    return lax.psum(kept, axis)


def contract(form, left_side, right_side):
    return jnp.einsum(form, left_side, right_side, precision=HIGHEST_PRECISION)


def contract_score(form, left_side, right_side):
    return jnp.einsum(form, left_side, right_side, precision=SCORE_PRECISION)


def apply_map(state_now, state_map):
    return contract("bhvk,bhkj->bhvj", state_now, state_map)


def local_pass(
    acceptance_gate,
    logarithmic_fade_factor,
    probe_matrix,
    payload_matrix,
    erasure_vector,
    inplace_update_step,
):
    symbol_entries, feature_total = acceptance_gate.shape
    blocks = symbol_entries // BLOCK
    group_total = feature_total // GROUP_DIMENSION

    def heads_first(array):
        return jnp.transpose(
            array.reshape(blocks, BLOCK, group_total, GROUP_DIMENSION), (0, 2, 1, 3)
        ).astype(jnp.float32)

    reader_in = heads_first(acceptance_gate)
    key_vals = heads_first(probe_matrix)
    values_h = heads_first(payload_matrix)
    log_step = -jnp.exp(heads_first(logarithmic_fade_factor))
    removal = heads_first(erasure_vector)
    kappa = (
        removal
        * lax.rsqrt(jnp.mean(removal * removal, -1, keepdims=True) + KEY_EPS)
        * GROUP_DIMENSION ** (-0.5)
    )
    away_dir = kappa * heads_first(inplace_update_step)
    row_ids = lax.broadcasted_iota(jnp.int32, (BLOCK, BLOCK), 0)
    col_ids = lax.broadcasted_iota(jnp.int32, (BLOCK, BLOCK), 1)
    inclusive = (row_ids >= col_ids).astype(jnp.float32)
    strict = (row_ids > col_ids).astype(jnp.float32)
    cumulative = jnp.cumsum(log_step, axis=2)
    before = cumulative - log_step
    toward_dec = -kappa * jnp.exp(before)
    reader_dec = reader_in * jnp.exp(cumulative)
    away_inv = away_dir * jnp.exp(-cumulative)
    keys_inv = key_vals * jnp.exp(-cumulative)
    gamma_end = jnp.exp(cumulative[:, :, -1])
    query_sides = jnp.concatenate([toward_dec, reader_dec], 2)
    key_sides = jnp.concatenate([away_inv, keys_inv], 2)
    scores = contract_score("nhtc,nhsc->nhts", query_sides, key_sides)
    mix_away = scores[:, :, :BLOCK, :BLOCK] * strict
    mix_keys = scores[:, :, :BLOCK, BLOCK:] * strict
    read_away = scores[:, :, BLOCK:, :BLOCK] * inclusive
    read_keys = scores[:, :, BLOCK:, BLOCK:] * inclusive
    known_side = jnp.concatenate(
        [toward_dec, contract_score("nhts,nhsc->nhtc", mix_keys, values_h)], -1
    )
    system = jnp.eye(BLOCK, dtype=jnp.float32) - mix_away
    solved = lax.linalg.triangular_solve(
        system, known_side, left_side=True, lower=True, unit_diagonal=True
    )
    from_state = solved[..., :GROUP_DIMENSION]
    from_values = solved[..., GROUP_DIMENSION:]
    unit_map = jnp.eye(GROUP_DIMENSION, dtype=jnp.float32)
    transition = (unit_map + contract("nhsk,nhsj->nhkj", from_state, away_inv)) * gamma_end[
        :, :, None, :
    ]
    contribution = (
        contract("nhsv,nhsj->nhvj", from_values, away_inv)
        + contract("nhsv,nhsj->nhvj", values_h, keys_inv)
    ) * gamma_end[:, :, None, :]
    reader = reader_dec + contract_score("nhts,nhsk->nhtk", read_away, from_state)
    within_split = contract_score("nhts,nhsv->nhtv", read_away, from_values) + contract_score(
        "nhts,nhsv->nhtv", read_keys, values_h
    )

    def advance_block(carried, pieces):
        map_so_far, add_so_far = carried
        step_map, step_add = pieces
        updated = (
            contract("hmk,hkj->hmj", map_so_far, step_map),
            contract("hvk,hkj->hvj", add_so_far, step_map) + step_add,
        )
        return (updated, (map_so_far, add_so_far))

    initial = (
        jnp.broadcast_to(unit_map, (group_total, GROUP_DIMENSION, GROUP_DIMENSION)),
        jnp.zeros((group_total, GROUP_DIMENSION, GROUP_DIMENSION), jnp.float32),
    )
    totals, priors = lax.scan(advance_block, initial, (transition, contribution))
    lifted_state = contract("nhtk,nhmk->nhtm", reader, priors[0])
    within_split = within_split + contract("nhtk,nhvk->nhtv", reader, priors[1])
    return (lifted_state, within_split, totals[1], totals[0])


def finish_output(
    lifted_state,
    within_split,
    incoming_state,
    acceptance_gate,
    probe_matrix,
    payload_matrix,
    extra_probe_factor,
    group_scaling_factor,
):
    symbol_entries, feature_total = acceptance_gate.shape
    group_total = feature_total // GROUP_DIMENSION
    result = within_split + contract("nhtm,hvm->nhtv", lifted_state, incoming_state)
    result = jnp.transpose(result, (0, 2, 1, 3)).reshape(
        symbol_entries, group_total, GROUP_DIMENSION
    )
    average = jnp.mean(result, -1, keepdims=True)
    centered = result - average
    spread = jnp.mean(centered * centered, -1, keepdims=True)
    standardized_result = (
        centered
        * lax.rsqrt(spread + NORM_EPS)
        * group_scaling_factor.reshape(group_total, GROUP_DIMENSION)
    )
    receptance_per_head = acceptance_gate.astype(jnp.float32).reshape(
        symbol_entries, group_total, GROUP_DIMENSION
    )
    key_per_head = probe_matrix.astype(jnp.float32).reshape(
        symbol_entries, group_total, GROUP_DIMENSION
    )
    value_per_head = payload_matrix.astype(jnp.float32).reshape(
        symbol_entries, group_total, GROUP_DIMENSION
    )
    extra_result = (
        jnp.sum(
            receptance_per_head
            * key_per_head
            * extra_probe_factor.reshape(group_total, GROUP_DIMENSION),
            -1,
            keepdims=True,
        )
        * value_per_head
    )
    return (
        (standardized_result + extra_result)
        .reshape(symbol_entries, feature_total)
        .astype(jnp.bfloat16)
    )


def on_device(
    acceptance_gate,
    logarithmic_fade_factor,
    probe_matrix,
    payload_matrix,
    erasure_vector,
    inplace_update_step,
    extra_probe_factor,
    group_scaling_factor,
):
    lifted_state, within_split, local_add, local_map = jax.vmap(local_pass)(
        acceptance_gate,
        logarithmic_fade_factor,
        probe_matrix,
        payload_matrix,
        erasure_vector,
        inplace_update_step,
    )
    members = lax.axis_size("seq")
    nothing = jnp.zeros_like(local_add)

    def relay(turn_index, carried):
        incoming = passed_along(carried[1], "seq", 1)
        return (incoming, apply_map(incoming, local_map) + local_add)

    incoming_state, leaving = lax.fori_loop(0, members - 1, relay, (nothing, local_add))
    closing = broadcast(leaving, "seq", members - 1)
    series_entries = closing.shape[0]
    flat_state = closing.reshape(series_entries, -1, GROUP_DIMENSION)
    slice_rows = flat_state.shape[1] // members
    final_state = lax.dynamic_slice_in_dim(
        flat_state, lax.axis_index("seq") * slice_rows, slice_rows, 1
    )
    blended_signal = jax.vmap(finish_output, in_axes=(0, 0, 0, 0, 0, 0, None, None))(
        lifted_state,
        within_split,
        incoming_state,
        acceptance_gate,
        probe_matrix,
        payload_matrix,
        extra_probe_factor,
        group_scaling_factor,
    )
    return (blended_signal, final_state)


def solution(mesh):
    in_specs = (
        P(("groups", "dp"), "seq", None),
        P(("groups", "dp"), "seq", None),
        P(("groups", "dp"), "seq", None),
        P(("groups", "dp"), "seq", None),
        P(("groups", "dp"), "seq", None),
        P(("groups", "dp"), "seq", None),
        P(),
        P(),
    )
    out_specs = (P(("groups", "dp"), "seq", None), P(("groups", "dp"), "seq", None))
    return jax.shard_map(
        on_device, mesh=mesh, in_specs=in_specs, out_specs=out_specs, check_vma=False
    )
```

profile of v0, /device:TPU:0, one launch (start us, length us, event | category | flops | bytes accessed | tf_op | source)
XLA Modules:
  0.0 385.0 jit_solution(7529248392724634668)
XLA Ops:
  7.3 1.1 exponential_negate_fusion
  8.3 0.4 reshape.388
  8.8 0.4 copy.89
  9.2 1.7 copy.90
  10.9 1.5 fusion.73
  12.4 1.5 copy.91
  13.9 0.4 reshape.389
  14.4 1.5 copy.96
  15.9 1.6 reshape.387
  17.5 1.8 copy.87
  19.6 1.0 copy-done.30
  20.8 1.9 reshape.385
  22.7 1.2 copy.92
  23.9 1.8 reshape.383
  26.0 0.3 reshape.368
  26.4 0.3 copy-done.20
  26.8 3.7 fusion.48
  30.6 2.4 convolution_bitcast_fusion.4
  32.9 3.0 convolution_bitcast_fusion.2
  35.9 2.0 convolution_bitcast_fusion.5
  37.9 1.6 fusion.34
  39.5 198.0 %custom-call.3 = f32[1,2,20,1,64,64]{4,5,3,2,1,0:T(8,128)} custom-call(f32[1,2,20,1,64,64]{5,4,3,2,1,0:T(8,128)} %fusion.34), custom_call_target="InvertDiagBlocksLowerTriangular" | custom-call | tf_op jit(solution)/shard_map/vmap()/triangular_solve | solution.py:89
  237.5 7.0 %fusion.19 = f32[1,2,20,64,128]{4,3,2,1,0:T(8,128)S(1)} fusion(f32[1,2,20,64,64]{3,4,2,1,0:T(8,128)} %convolution_bitcast_fusion.5, f32[1,2,20,64,64]{3,4,2,1,0:T(8,128)S(1)} %copy-done.12, f32[1,2,20,1,64,64]{4,5,3,2,1,0:T(8,128)} %custom-call.3), kind=kOutput, calls=%fused_computation.34 | convolution fusion | flops 251985920 | bytes 3276800 | tf_op jit(solution)/shard_map/vmap()/triangular_solve | solution.py:89
  244.6 2.4 fusion.20
  247.0 3.9 %fusion.21 = f32[2,1,20,64,64]{4,3,2,0,1:T(8,128)} fusion(f32[2,20,64,64]{3,2,1,0:T(8,128)S(1)} %copy-done.15, f32[1,2,20,64,64]{3,4,2,1,0:T(8,128)S(1)} %get-tuple-element.141, f32[1,2,20,64,128]{4,3,2,1,0:T(8,128)S(1)} %fusion.19, f32[2,20,64]{2,1,0:T(8,128)S(1)} %fusion.69), kind=kOutput, calls=%fused_computation.36 | convolution fusion | flops 126156800 | bytes 3287040 | tf_op jit(solution)/shard_map/vmap(nhsv,nhsj->nhvj)/dot_general | solution.py:28
  250.9 0.9 broadcast.123.clone
  251.8 13.4 %while.30 = (s32[]{:T(128)}, f32[1,20,64,64]{2,3,1,0:T(8,128)S(1)}, f32[1,20,64,64]{2,3,1,0:T(8,128)}, f32[2,1,20,64,64]{3,4,2,1,0:T(8,128)}, f32[2,1,20,64,64]{...) while((s32[]{:T(128)}, f32[1,20,64,64]{2,3,1,0:T(8,128)S(1)}, ...), condition=%wide.region_3.4_spmd.clone, body=%wide.region_2.3_spmd.sunk.clone | while | flops 125911040 | bytes 23593228 | solution.py:120
  251.8 1.2 copy.215
  253.3 0.4 copy-done.27
  253.9 2.1 convolution_bitcast_fusion.9
  256.4 2.0 fusion.97
  258.5 1.2 copy.215
  260.0 0.4 copy-done.27
  260.6 2.1 convolution_bitcast_fusion.9
  263.2 2.0 fusion.97
  265.2 1.3 copy.120
  266.9 65.4 %while.31 = (s32[]{:T(128)}, f32[1,20,64,64]{3,2,1,0:T(8,128)}, f32[1,20,64,64]{3,2,1,0:T(8,128)S(1)}, f32[1,20,64,64]{3,2,1,0:T(8,128)S(1)}, f32[1,20,64,64]{3,2,1,0:T(8,128)S(1)}) while((s32[]{:T(128)}, f32[1,20,64,64]{3,2,1,0:T(8,128)}, f32[1,20,64,64]{3,2,1,0:T(8,128)S(1)}, f32[1,20,64,64]{3,2,1,0:T(8,128)S(1)}, ...), condition=%wide.region_5.6_spmd.clone, body=%wide.region_4.5_spmd.sunk.clone | while | flops 62996480 | bytes 3932289 | solution.py:201
  266.9 5.1 %collective-permute-start = (f32[1,20,64,64]{3,2,1,0:T(8,128)S(1)}, f32[1,20,64,64]{3,2,1,0:T(8,128)S(1)}, u32[]{:S(2)}, u32[]{:S(2)}) collective-permute-start(f32[1,20,64,64]{3,2,1,0:T(8,128)S(1)} %get-tuple-element.284), channel_id=1, source_target_pairs={{0,4},{4,8},{8,12},{1,5},{5,9},{9,13},{2,6},{6,10},{10,14},{3,7},{... | collective-permute-start | bytes 983048 | tf_op jit(solution)/shard_map/while/body/eval_jaxpr/ppermute | solution.py:19
  272.0 13.9 %collective-permute-done = f32[1,20,64,64]{3,2,1,0:T(8,128)S(1)} collective-permute-done((f32[1,20,64,64]{3,2,1,0:T(8,128)S(1)}, f32[1,20,64,64]{3,2,1,0:T(8,128)S(1)}, u32[]{:S(2)}, u32[]{:S(2)}) %collective-permute-start) | collective-permute-done | bytes 327712 | tf_op jit(solution)/shard_map/while/body/eval_jaxpr/ppermute | solution.py:19
  285.9 0.8 fusion.100
  286.8 4.4 %collective-permute-start = (f32[1,20,64,64]{3,2,1,0:T(8,128)S(1)}, f32[1,20,64,64]{3,2,1,0:T(8,128)S(1)}, u32[]{:S(2)}, u32[]{:S(2)}) collective-permute-start(f32[1,20,64,64]{3,2,1,0:T(8,128)S(1)} %get-tuple-element.284), channel_id=1, source_target_pairs={{0,4},{4,8},{8,12},{1,5},{5,9},{9,13},{2,6},{6,10},{10,14},{3,7},{... | collective-permute-start | bytes 983048 | tf_op jit(solution)/shard_map/while/body/eval_jaxpr/ppermute | solution.py:19
  291.2 13.1 %collective-permute-done = f32[1,20,64,64]{3,2,1,0:T(8,128)S(1)} collective-permute-done((f32[1,20,64,64]{3,2,1,0:T(8,128)S(1)}, f32[1,20,64,64]{3,2,1,0:T(8,128)S(1)}, u32[]{:S(2)}, u32[]{:S(2)}) %collective-permute-start) | collective-permute-done | bytes 327712 | tf_op jit(solution)/shard_map/while/body/eval_jaxpr/ppermute | solution.py:19
  304.3 0.8 fusion.100
  305.1 4.4 %collective-permute-start = (f32[1,20,64,64]{3,2,1,0:T(8,128)S(1)}, f32[1,20,64,64]{3,2,1,0:T(8,128)S(1)}, u32[]{:S(2)}, u32[]{:S(2)}) collective-permute-start(f32[1,20,64,64]{3,2,1,0:T(8,128)S(1)} %get-tuple-element.284), channel_id=1, source_target_pairs={{0,4},{4,8},{8,12},{1,5},{5,9},{9,13},{2,6},{6,10},{10,14},{3,7},{... | collective-permute-start | bytes 983048 | tf_op jit(solution)/shard_map/while/body/eval_jaxpr/ppermute | solution.py:19
  309.5 12.2 %collective-permute-done = f32[1,20,64,64]{3,2,1,0:T(8,128)S(1)} collective-permute-done((f32[1,20,64,64]{3,2,1,0:T(8,128)S(1)}, f32[1,20,64,64]{3,2,1,0:T(8,128)S(1)}, u32[]{:S(2)}, u32[]{:S(2)}) %collective-permute-start) | collective-permute-done | bytes 327712 | tf_op jit(solution)/shard_map/while/body/eval_jaxpr/ppermute | solution.py:19
  321.7 0.8 fusion.100
  332.3 0.9 copy-done.23
  333.2 1.0 broadcast_select_fusion
  334.2 2.1 copy.158
  336.4 0.9 fusion.27
  337.3 0.4 copy-done.1
  337.7 0.4 copy-done.10
  338.1 1.2 fusion.25
  339.3 0.9 convert_multiply_fusion
  340.2 1.6 convolution_add_fusion.4
  341.9 2.3 fusion.40
  344.2 2.3 fusion.16
  346.6 3.9 %fusion.72 = (f32[2,64,20]{1,2,0:T(8,128)S(1)}, f32[1,2,64,20,64]{2,4,3,1,0:T(8,128)S(1)}) fusion(f32[1,2,20,64,64]{3,4,2,1,0:T(8,128)S(1)} %fusion.16, f32[2,20,64,64]{3,2,0,1:T(8,128)S(1)} %fusion.40, f32[1,20,64,64]{3,2,1,0:T(8,128)S(1)} %copy-done.6), kind=kOutput, calls=%fused_computation.118 | convolution fusion | flops 126154240 | bytes 2304000 | tf_op jit(solution)/shard_map/vmap(nhtm,hvm->nhtv)/dot_general | solution.py:28
  350.5 1.0 copy.126
  351.9 0.7 reshape.380
  353.2 0.3 fusion.55
  353.4 0.9 copy.131
  354.4 21.9 %all-reduce.2.cloned.1.call-done = f32[1,1280,64]{1,2,0:T(8,128)} async-done(((f32[1,1280,64]{1,2,0:T(8,128)}), f32[1,1280,64]{1,2,0:T(8,128)}) %all-reduce.2.cloned.1.call-update) | async-done | bytes 327696 | tf_op jit(solution)/shard_map/psum | solution.py:24
  376.3 1.6 constant_dynamic-slice_fusion.1
  (116 shorter events, 4.1 us)
Async XLA Ops:
  7.2 369.1 %all-reduce.2.cloned.1.call-start = ((), (), s32[]{:S(2)}) async-start(), calls=%async_computation | async-start | bytes 655360 | tf_op jit(solution)/shard_map/psum | solution.py:24
  12.4 1.5 copy-start.32
  14.4 1.5 copy-start.33
  19.4 3.4 copy-start.8
  19.4 1.2 copy-start.30
  20.8 5.0 %copy-start.16 = (bf16[1,128,1280]{1,2,0:T(8,128)(2,1)}, bf16[1,128,1280]{1,2,0:T(8,128)(2,1)S(1)}, u32[]{:S(2)}) copy-start(bf16[1,128,1280]{1,2,0:T(8,128)(2,1)S(1)} %copy.98) | copy-start | bytes 983044
  23.9 2.4 copy-start.18
  23.9 1.9 copy-start.31
  26.0 0.7 copy-start.20
  26.3 9.6 %copy-start.13 = (bf16[1,2,64,20,64]{2,1,4,3,0:T(2,128)(2,1)}, bf16[1,2,64,20,64]{2,1,4,3,0:T(2,128)(2,1)S(1)}, u32[]{:S(2)}) copy-start(bf16[1,2,64,20,64]{2,1,4,3,0:T(2,128)(2,1)S(1)} %reshape.368) | copy-start | bytes 983044
  30.5 2.4 copy-start.9
  30.5 2.4 copy-start.11
  35.9 2.0 copy-start.2
  37.9 199.6 %copy-start.12 = (f32[1,2,20,64,64]{3,4,2,1,0:T(8,128)S(1)}, f32[1,2,20,64,64]{3,4,2,1,0:T(8,128)}, u32[]{:S(2)}) copy-start(f32[1,2,20,64,64]{3,4,2,1,0:T(8,128)} %copy-done.11) | copy-start | bytes 1966084
  244.5 2.4 copy-start
  244.5 2.4 copy-start.15
  251.8 1.5 copy-start.24
  251.8 1.9 copy-start.27
  253.8 2.1 copy-start.25
  253.9 2.1 copy-start.28
  253.9 2.3 copy-start.7
  256.4 2.1 copy-start.4
  258.5 1.5 copy-start.24
  258.5 1.9 copy-start.27
  260.6 2.1 copy-start.25
  260.6 2.1 copy-start.28
  260.6 2.3 copy-start.7
  263.2 2.1 copy-start.4
  266.8 69.5 %copy-start.14 = (bf16[1,2,64,20,64]{2,1,4,3,0:T(2,128)(2,1)S(1)}, bf16[1,2,64,20,64]{2,1,4,3,0:T(2,128)(2,1)}, u32[]{:S(2)}) copy-start(bf16[1,2,64,20,64]{2,1,4,3,0:T(2,128)(2,1)} %copy-done.13) | copy-start | bytes 983044
  266.9 19.1 %collective-permute-start = (f32[1,20,64,64]{3,2,1,0:T(8,128)S(1)}, f32[1,20,64,64]{3,2,1,0:T(8,128)S(1)}, u32[]{:S(2)}, u32[]{:S(2)}) collective-permute-start(f32[1,20,64,64]{3,2,1,0:T(8,128)S(1)} %get-tuple-element.284), channel_id=1, source_target_pairs={{0,4},{4,8},{8,12},{1,5},{5,9},{9,13},{2,6},{6,10},{10,14},{3,7},{... | collective-permute-start | bytes 983048 | tf_op jit(solution)/shard_map/while/body/eval_jaxpr/ppermute | solution.py:19
  285.9 0.8 copy-start.5
  286.8 17.5 %collective-permute-start = (f32[1,20,64,64]{3,2,1,0:T(8,128)S(1)}, f32[1,20,64,64]{3,2,1,0:T(8,128)S(1)}, u32[]{:S(2)}, u32[]{:S(2)}) collective-permute-start(f32[1,20,64,64]{3,2,1,0:T(8,128)S(1)} %get-tuple-element.284), channel_id=1, source_target_pairs={{0,4},{4,8},{8,12},{1,5},{5,9},{9,13},{2,6},{6,10},{10,14},{3,7},{... | collective-permute-start | bytes 983048 | tf_op jit(solution)/shard_map/while/body/eval_jaxpr/ppermute | solution.py:19
  304.3 0.8 copy-start.5
  305.1 16.6 %collective-permute-start = (f32[1,20,64,64]{3,2,1,0:T(8,128)S(1)}, f32[1,20,64,64]{3,2,1,0:T(8,128)S(1)}, u32[]{:S(2)}, u32[]{:S(2)}) collective-permute-start(f32[1,20,64,64]{3,2,1,0:T(8,128)S(1)} %get-tuple-element.284), channel_id=1, source_target_pairs={{0,4},{4,8},{8,12},{1,5},{5,9},{9,13},{2,6},{6,10},{10,14},{3,7},{... | collective-permute-start | bytes 983048 | tf_op jit(solution)/shard_map/while/body/eval_jaxpr/ppermute | solution.py:19
  321.7 0.8 copy-start.5
  332.3 0.9 copy-start.23
  333.2 3.1 copy-start.3
  336.4 1.3 copy-start.1
  336.4 1.7 copy-start.10
  338.1 1.2 copy-start.17
  338.1 1.3 copy-start.19
  340.2 1.6 copy-start.29
  341.9 2.3 copy-start.26
  344.2 2.3 copy-start.6
  351.8 0.8 copy-start.35
  351.8 1.1 copy-start.22
  351.8 1.3 copy-start.21
  351.9 1.3 copy-start.34
Sparse Core Ops, SparseCore 0:
  336.4 39.8 all-reduce.1
where the time goes:
time: 389 us; the launch traced here: 385 us
  other arithmetic  209 us (54%)
  waiting for transfers between devices  61.2 us (16%)
  matrix products  43.5 us (11%)
  local copies, waits for them, and re-layouts  32.7 us (8%)
  between operations  14.8 us (4%)
  starting transfers between devices  14 us (4%)
  loops' own time  9.93 us (3%)
    another operation x4, other arithmetic, local_pass(): lax.linalg.triangular_solve(system, known_side, left_side=True, lower=Tru...  200 us
    ppermute x3, waiting for transfers between devices, passed_along(): return lax.ppermute(shard, axis, pairs)  39.2 us
    dot_general x13, matrix products, contract(): return jnp.einsum(form, left_side, right_side, precision=HIGHEST_PRECISION)  27.7 us
    psum x1, waiting for transfers between devices, broadcast(): return lax.psum(kept, axis)  21.9 us
    ppermute x3, starting transfers between devices, passed_along(): return lax.ppermute(shard, axis, pairs)  14 us
    another operation x1, loops' own time, on_device(): lax.fori_loop(0, members - 1, relay, (nothing, local_add))  9.79 us
    convert_element_type x6, local copies, waits for them, and re-layouts, heads_first(): return jnp.transpose(array.reshape(blocks, BLOCK, group_total, GROUP_DIME...  9.15 us
    dot_general x5, matrix products, contract_score(): return jnp.einsum(form, left_side, right_side, precision=SCORE_PRECISION)  8.73 us
  transfers between devices with their start and end apart: 4, of which 4 were waited for; matrix products, arithmetic and copies ran while one was open for 4% of the time, Pallas kernels for 0%

commit v1 on v0

v1 whole, which is shorter than its diff:
```python
import functools

import jax
import jax.numpy as jnp
from jax import lax
from jax.experimental import pallas as pl
from jax.experimental.pallas import tpu as pltpu
from jax.sharding import PartitionSpec as P

GROUP_DIMENSION = 64
PAIR = 2 * GROUP_DIMENSION
KEY_EPS = 1e-05
NORM_EPS = 0.00064
STEP_PAIRS = 2

F32 = jnp.float32
BF16 = jnp.bfloat16


def mm(left, right):
    return jnp.dot(left, right, preferred_element_type=F32)


def split(x):
    high = x.astype(BF16)
    return high, (x - high.astype(F32)).astype(BF16)


def side(*parts):
    return jnp.concatenate(parts, axis=1)


def stack(*parts):
    return jnp.concatenate(parts, axis=0)


def mm3(left, right):
    lh, ll = left
    rh, rl = right
    return mm(side(lh, ll), stack(rh, rh)) + mm(lh, rl)


def iota(shape, axis):
    return lax.broadcasted_iota(jnp.int32, shape, axis)


def group_ones():
    same = (iota((PAIR, PAIR), 0) // GROUP_DIMENSION) == (
        iota((PAIR, PAIR), 1) // GROUP_DIMENSION
    )
    ones = same.astype(F32).astype(BF16)
    return stack(ones, ones)


def group_sums(x, ones):
    parts = []
    for p in range(x.shape[1] // PAIR):
        high, low = split(x[:, p * PAIR : (p + 1) * PAIR])
        parts.append(mm(side(high, low), ones))
    return side(*parts)


def block_diagonal(x):
    top, bottom = x[:GROUP_DIMENSION], x[GROUP_DIMENSION:]
    none = jnp.zeros_like(top)
    return stack(side(top, none), side(none, bottom))


def scores(first, second, query, late):
    qh, ql = (block_diagonal(q) for q in query)
    out_first = mm3(first, (qh, ql))
    out_second = mm3(second, (qh * late, ql * late))
    return out_first, out_second


def local_kernel(
    owners,
    reader_ref,
    fade_ref,
    key_ref,
    value_ref,
    removal_ref,
    rate_ref,
    extra_ref,
    *rest,
):
    send_refs = rest[:owners]
    lift_high_ref, lift_low_ref, within_ref, bonus_ref, held, sems = rest[owners:]
    step = pl.program_id(0)
    me = lax.axis_index("seq")
    tokens = reader_ref.shape[0]
    half = tokens // 2
    width = reader_ref.shape[1]
    pairs = width // PAIR
    per_owner = held.shape[1]

    row = iota((tokens, tokens), 0)
    col = iota((tokens, tokens), 1)
    lower = (row >= col).astype(F32).astype(BF16)
    ones = group_ones()
    late_lane = iota((PAIR, 2 * tokens), 1) % tokens
    late = (late_lane >= half).astype(F32).astype(BF16)

    reader = reader_ref[...].astype(F32)
    key = key_ref[...].astype(F32)
    value = value_ref[...].astype(F32)
    removal = removal_ref[...].astype(F32)
    rate = rate_ref[...].astype(F32)
    log_step = -jnp.exp(fade_ref[...].astype(F32))

    high, low = split(log_step)
    rest_low = (log_step - high.astype(F32) - low.astype(F32)).astype(BF16)
    cum = mm(side(lower, lower), stack(high, low)) + mm(lower, rest_low)
    middle = cum[half - 1 : half]
    end = cum[tokens - 1 : tokens]
    before = cum - log_step

    norm = group_sums(removal * removal, ones) * (1.0 / GROUP_DIMENSION)
    kappa = removal * lax.rsqrt(norm + KEY_EPS) * GROUP_DIMENSION ** (-0.5)

    inverse = jnp.exp(middle - cum)
    away = kappa * rate * inverse
    keys = key * inverse
    to_end = jnp.exp(end - middle)
    gamma_end = jnp.exp(end)
    toward_mid = -kappa * jnp.exp(before - middle)
    toward_abs = -kappa * jnp.exp(before)
    reader_mid = reader * jnp.exp(cum - middle)
    reader_abs = reader * jnp.exp(cum)

    bonus = group_sums(reader * key * extra_ref[...], ones)
    bonus_ref[...] = bonus * value

    lane = iota((GROUP_DIMENSION, PAIR), 1)
    sub = iota((GROUP_DIMENSION, PAIR), 0)

    for p in range(pairs):
        cut = slice(p * PAIR, (p + 1) * PAIR)
        away_p = split(away[:, cut])
        keys_p = split(keys[:, cut])
        first = tuple(stack(a[:half], k[:half]) for a, k in zip(away_p, keys_p))
        second = tuple(stack(a[half:], k[half:]) for a, k in zip(away_p, keys_p))
        t_mid = split(toward_mid[:, cut].T)
        r_mid = split(reader_mid[:, cut].T)
        t_abs = toward_abs[:, cut].T
        r_abs = reader_abs[:, cut].T
        value_t = value[:, cut].T.astype(BF16)
        mix_first, mix_second = scores(first, second, t_mid, late)
        read_first, read_second = scores(first, second, r_mid, late)
        away_end = split(away[:, cut] * to_end[:, cut])
        keys_end = split(keys[:, cut] * to_end[:, cut])

        for i in range(2):
            lanes = slice(i * tokens, (i + 1) * tokens)
            rows = slice(i * GROUP_DIMENSION, (i + 1) * GROUP_DIMENSION)

            def pick(a, b, top, keep):
                part = slice(0, half) if top else slice(half, 2 * half)
                return jnp.where(keep, stack(a[part, lanes], b[part, lanes]), 0.0)

            power = pick(mix_first, mix_second, True, row < col)
            mix_keys = pick(mix_first, mix_second, False, row < col)
            read_away = pick(read_first, read_second, True, row <= col)
            read_keys = pick(read_first, read_second, False, row <= col)
            value_h = value_t[rows]
            value_two = side(value_h, value_h)

            mk_high, mk_low = split(mix_keys)
            solved = stack(t_abs[rows], mm(value_two, stack(mk_high, mk_low)))
            ps = split(power)
            ws = split(solved)
            out = mm3(tuple(stack(w, q) for w, q in zip(ws, ps)), ps)
            solved = solved + out[:tokens]
            ps = split(out[tokens:])
            solved = solved + mm3(split(solved), ps)
            power = mm(ps[0], ps[0]).astype(BF16)
            reach = 4
            while reach < tokens:
                if reach * 2 < tokens:
                    out = mm(stack(solved.astype(BF16), power), power)
                    solved = solved + out[:tokens]
                    power = out[tokens:].astype(BF16)
                else:
                    solved = solved + mm(solved.astype(BF16), power)
                reach *= 2

            ws = split(solved)
            ended = mm3(ws, away_end)
            stay = jnp.where(
                lane == sub + i * GROUP_DIMENSION, gamma_end[:, cut], 0.0
            )
            state_map = ended[:GROUP_DIMENSION] + stay
            state_add = ended[GROUP_DIMENSION:] + mm(value_two, stack(*keys_end))
            if i == 0:
                state_add = pltpu.roll(state_add, GROUP_DIMENSION, 1)
            else:
                state_map = pltpu.roll(state_map, GROUP_DIMENSION, 1)
            both = jnp.where(lane < GROUP_DIMENSION, state_map, state_add)
            head = (step * pairs + p) * 2 + i
            slot = lax.rem(head // per_owner - me % owners + owners, owners)
            held[slot, lax.rem(head, per_owner)] = both

            read = mm3(ws, split(read_away))
            rk_high, rk_low = split(read_keys)
            within = read[GROUP_DIMENSION:] + mm(value_two, stack(rk_high, rk_low))
            lift_high, lift_low = split(r_abs[rows] + read[:GROUP_DIMENSION])
            at = slice(p * PAIR + i * GROUP_DIMENSION, p * PAIR + (i + 1) * GROUP_DIMENSION)
            lift_high_ref[at] = lift_high
            lift_low_ref[at] = lift_low
            within_ref[at] = within

    @pl.when(step == pl.num_programs(0) - 1)
    def _():
        copies = [
            pltpu.make_async_copy(held.at[k], send_refs[k], sems.at[k])
            for k in range(owners)
        ]
        for copy in copies:
            copy.start()
        for copy in copies:
            copy.wait()


def local_pass(owners, reader, fade, key, value, removal, rate, extra):
    tokens, features = reader.shape
    heads = features // GROUP_DIMENSION
    per_owner = heads // owners
    width = STEP_PAIRS * PAIR
    natural = pl.BlockSpec((tokens, width), lambda g: (0, g))
    turned = pl.BlockSpec((width, tokens), lambda g: (g, 0))
    vector = pl.BlockSpec((1, width), lambda g: (0, g))
    block = (per_owner, GROUP_DIMENSION, PAIR)
    out = pl.pallas_call(
        functools.partial(local_kernel, owners),
        grid=(features // width,),
        in_specs=[natural] * 6 + [vector],
        out_specs=[pl.BlockSpec(memory_space=pl.ANY)] * owners
        + [turned, turned, turned, natural],
        out_shape=[jax.ShapeDtypeStruct(block, F32)] * owners
        + [
            jax.ShapeDtypeStruct((features, tokens), BF16),
            jax.ShapeDtypeStruct((features, tokens), BF16),
            jax.ShapeDtypeStruct((features, tokens), F32),
            jax.ShapeDtypeStruct((tokens, features), F32),
        ],
        scratch_shapes=[
            pltpu.VMEM((owners,) + block, F32),
            pltpu.SemaphoreType.DMA((owners,)),
        ],
        name="local_pass",
    )(reader, fade, key, value, removal, rate, extra)
    return out[:owners], out[owners:]


def pack_rows(state):
    rows = state.shape[0] // 2
    return side(state[:rows], state[rows:])


def chain_kernel(owners, *refs):
    got_refs = refs[:owners]
    state_refs = refs[owners : 2 * owners]
    final_ref, ranges, states = refs[2 * owners :]
    me = lax.axis_index("seq")
    per_owner = got_refs[0].shape[0]
    for k in range(owners):
        ranges[lax.rem(me - k + owners, owners)] = got_refs[k][...]
    d = GROUP_DIMENSION
    current = []
    for q in range(per_owner):
        states[0, q] = jnp.zeros((d // 2, PAIR), F32)
        current.append(ranges[0, q][:, d:])
    for i in range(1, owners + 1):
        for q in range(per_owner):
            if i < owners:
                states[i, q] = pack_rows(current[q])
                both = ranges[i, q]
                maps = split(both)
                moved = mm3(split(current[q]), maps)[:, :d]
                current[q] = moved + both[:, d:]
            else:
                final_ref[q * d : (q + 1) * d, :] = current[q]
    for k in range(owners):
        state_refs[k][...] = states[lax.rem(me + k, owners)]


def chain(got):
    owners = len(got)
    per_owner = got[0].shape[0]
    block = (per_owner, GROUP_DIMENSION // 2, PAIR)
    rows = per_owner * GROUP_DIMENSION
    whole = pl.BlockSpec(memory_space=pltpu.VMEM)
    out = pl.pallas_call(
        functools.partial(chain_kernel, owners),
        in_specs=[whole] * owners,
        out_specs=[whole] * (owners + 1),
        out_shape=[jax.ShapeDtypeStruct(block, F32)] * owners
        + [jax.ShapeDtypeStruct((rows, GROUP_DIMENSION), F32)],
        scratch_shapes=[
            pltpu.VMEM((owners,) + got[0].shape, F32),
            pltpu.VMEM((owners,) + block, F32),
        ],
        name="chain",
    )(*got)
    return out[:owners], out[owners]


def finish_kernel(owners, *refs):
    state_refs = refs[:owners]
    lift_high_ref, lift_low_ref, within_ref, bonus_ref, gain_ref = refs[
        owners : owners + 5
    ]
    out_ref, states = refs[owners + 5 :]
    step = pl.program_id(0)
    me = lax.axis_index("seq")
    per_owner = state_refs[0].shape[0]
    width = out_ref.shape[1]
    d = GROUP_DIMENSION

    @pl.when(step == 0)
    def _():
        for k in range(owners):
            states[lax.rem(me % owners - k + owners, owners)] = state_refs[k][...]

    lane = iota((d // 2, PAIR), 1)
    for p in range(width // PAIR):
        normed = []
        for i in range(2):
            head = (step * (width // PAIR) + p) * 2 + i
            packed = states[head // per_owner, lax.rem(head, per_owner)]
            state = split(
                stack(
                    jnp.where(lane < d, packed, 0.0),
                    jnp.where(lane >= d, packed, 0.0),
                )
            )
            at = slice(p * PAIR + i * d, p * PAIR + (i + 1) * d)
            high, low = lift_high_ref[at], lift_low_ref[at]
            result = within_ref[at] + mm3(
                state, (stack(high, high), stack(low, low))
            )
            average = jnp.mean(result, axis=0, keepdims=True)
            centered = result - average
            spread = jnp.mean(centered * centered, axis=0, keepdims=True)
            normed.append(centered * lax.rsqrt(spread + NORM_EPS))
        cut = slice(p * PAIR, (p + 1) * PAIR)
        turned = stack(*normed).T
        out_ref[:, cut] = (turned * gain_ref[:, cut] + bonus_ref[:, cut]).astype(BF16)


def finish(states, lift_high, lift_low, within, bonus, gain):
    owners = len(states)
    tokens, features = bonus.shape
    width = STEP_PAIRS * PAIR
    natural = pl.BlockSpec((tokens, width), lambda g: (0, g))
    turned = pl.BlockSpec((width, tokens), lambda g: (g, 0))
    vector = pl.BlockSpec((1, width), lambda g: (0, g))
    whole = pl.BlockSpec(memory_space=pltpu.VMEM)
    return pl.pallas_call(
        functools.partial(finish_kernel, owners),
        grid=(features // width,),
        in_specs=[whole] * owners + [turned, turned, turned, natural, vector],
        out_specs=natural,
        out_shape=jax.ShapeDtypeStruct((tokens, features), BF16),
        scratch_shapes=[pltpu.VMEM((owners,) + states[0].shape, F32)],
        name="finish",
    )(*states, lift_high, lift_low, within, bonus, gain)


def shifted(value, by, members):
    return lax.ppermute(value, "seq", [(i, (i + by) % members) for i in range(members)])


def relay_states(both, members):
    d = GROUP_DIMENSION
    local_map, local_add = both[:, :, :d], both[:, :, d:]

    def relay(_, carried):
        pairs = [(i, i + 1) for i in range(members - 1)]
        incoming = lax.ppermute(carried[1], "seq", pairs)
        moved = jnp.einsum(
            "hvk,hkj->hvj", incoming, local_map, precision=lax.Precision.HIGHEST
        )
        return (incoming, moved + local_add)

    first = (jnp.zeros_like(local_add), local_add)
    incoming, leaving = lax.fori_loop(0, members - 1, relay, first)
    here = lax.axis_index("seq")
    closing = lax.psum(jnp.where(here == members - 1, leaving, 0.0), "seq")
    closing = closing.reshape(-1, d)
    rows = closing.shape[0] // members
    final = lax.dynamic_slice_in_dim(closing, here * rows, rows, 0)
    packed = jnp.concatenate([incoming[:, : d // 2], incoming[:, d // 2 :]], axis=2)
    return packed, final


def on_device(reader, fade, key, value, removal, rate, extra, gain):
    members = lax.axis_size("seq")
    features = reader.shape[2]
    heads = features // GROUP_DIMENSION
    owners = members if heads % members == 0 else 1
    sends, parts = local_pass(
        owners,
        reader[0],
        fade[0],
        key[0],
        value[0],
        removal[0],
        rate[0],
        extra.reshape(1, features),
    )
    if owners > 1:
        got = [sends[0]] + [shifted(sends[k], k, members) for k in range(1, owners)]
        states, final = chain(got)
        states = [states[0]] + [
            shifted(states[k], k, members) for k in range(1, owners)
        ]
    else:
        packed, final = relay_states(sends[0], members)
        states = [packed]
    blended = finish(states, *parts, gain.reshape(1, features))
    return (blended[None], final[None])


def solution(mesh):
    tokens = P(("groups", "dp"), "seq", None)
    return jax.shard_map(
        on_device,
        mesh=mesh,
        in_specs=(tokens,) * 6 + (P(), P()),
        out_specs=(tokens, tokens),
        check_vma=False,
    )
```

time: 389 us -> 73.2 us (0.19)
  other arithmetic: 209 us -> 0 us
  waiting for transfers between devices: 61.2 us -> 12.8 us
  matrix products: 43.5 us -> 0 us
  Pallas kernels: 0 us -> 41.2 us
  local copies, waits for them, and re-layouts: 32.7 us -> 4.91 us
  between operations: 14.8 us -> 0.66 us
  loops' own time: 9.93 us -> 0 us
    another operation x8 -> x0, other arithmetic: 201 us -> none  [the longest x4 200 us: local_pass(): lax.linalg.triangular_solve(system, known_side, left_side=True, lower=Tru...]
    pallas_call x0 -> x3, Pallas kernels: none -> 41.2 us  [the longest x1 33.3 us: local_pass(): pl.pallas_call(functools.partial(local_kernel, owners), grid=(features //...]
    dot_general x18 -> x0, matrix products: 36.5 us -> none  [the longest x13 27.7 us: contract(): return jnp.einsum(form, left_side, right_side, precision=HIGHEST_PRECISION)]
    ppermute x3 -> x6, waiting for transfers between devices: 39.2 us -> 12.8 us  [shifted(): lax.ppermute(value, 'seq', [(i, (i + by) % members) for i in range(member...]
    psum x1 -> x0, waiting for transfers between devices: 21.9 us -> none  [broadcast(): return lax.psum(kept, axis)]
    another operation x2 -> x0, loops' own time: 9.93 us -> none  [the longest x1 9.79 us: on_device(): lax.fori_loop(0, members - 1, relay, (nothing, local_add))]
    convert_element_type x7 -> x0, local copies, waits for them, and re-layouts: 9.22 us -> none  [the longest x6 9.15 us: heads_first(): return jnp.transpose(array.reshape(blocks, BLOCK, group_total, GROUP_DIME...]
    another operation x1 -> x0, matrix products: 7.04 us -> none  [local_pass(): lax.linalg.triangular_solve(system, known_side, left_side=True, lower=Tru...]
  transfers between devices with their start and end apart: 4 -> 6, of which waited for: 4 -> 4; matrix products, arithmetic and copies ran while one was open for 4% -> 3% of each run, Pallas kernels for 0% -> 0%
where the time goes in v1:
time: 73.2 us; the launch traced here: 72.9 us
  Pallas kernels  41.2 us (56%)
  starting transfers between devices  13.3 us (18%)
  waiting for transfers between devices  12.8 us (17%)
  local copies, waits for them, and re-layouts  4.91 us (7%)
    pallas_call x1, Pallas kernels, local_pass(): pl.pallas_call(functools.partial(local_kernel, owners), grid=(features //...  33.3 us
    ppermute x6, starting transfers between devices, shifted(): lax.ppermute(value, 'seq', [(i, (i + by) % members) for i in range(member...  13.3 us
    ppermute x6, waiting for transfers between devices, shifted(): lax.ppermute(value, 'seq', [(i, (i + by) % members) for i in range(member...  12.8 us
    pallas_call x1, Pallas kernels, finish(): pl.pallas_call(functools.partial(finish_kernel, owners), grid=(features /...  5.12 us
    unnamed x15, local copies, waits for them, and re-layouts  3.03 us
    pallas_call x1, Pallas kernels, chain(): pl.pallas_call(functools.partial(chain_kernel, owners), in_specs=[whole]...  2.74 us
  transfers between devices with their start and end apart: 6, of which 4 were waited for; matrix products, arithmetic and copies ran while one was open for 3% of the time, Pallas kernels for 0%

profile of v1, /device:TPU:0, one launch (start us, length us, event | category | flops | bytes accessed | tf_op | source)
XLA Modules:
  0.0 72.9 jit_solution(9686337114947051363)
XLA Ops:
  0.6 1.3 %reshape.10.extra_ref = f32[1,1280]{1,0:T(1,128)} reshape(f32[1280]{0:T(1024)} %param.14) | data formatting | bytes 10240 | tf_op jit(solution)/shard_map/reshape | solution.py:410
  1.9 33.3 %local_pass.1 = (f32[5,64,128]{2,1,0:T(8,128)}, f32[5,64,128]{2,1,0:T(8,128)}, f32[5,64,128]{2,1,0:T(8,128)}, f32[5,64,128]{2,1,0:T(8,128)}, bf16[1280,128]{1,0:...) custom-call(bf16[128,1280]{1,0:T(8,128)(2,1)} %bitcast.8, ...), custom_call_target="tpu_custom_call" | custom-call | tf_op jit(solution)/shard_map/local_pass/pallas_call | solution.py:233
  35.3 3.1 %collective-permute-start = (f32[5,64,128]{2,1,0:T(8,128)}, f32[5,64,128]{2,1,0:T(8,128)S(1)}, u32[]{:S(2)}, u32[]{:S(2)}) collective-permute-start(f32[5,64,128]{2,1,0:T(8,128)} %get-tuple-element.16), channel_id=1, source_target_pairs={{0,4},{4,8},{8,12},{12,0},{1,5},{5,9},{9,13},{13,1},{2,6},{6,10},{... | collective-permute-start | bytes 491528 | tf_op jit(solution)/shard_map/ppermute | solution.py:371
  38.4 2.6 %collective-permute-start.1 = (f32[5,64,128]{2,1,0:T(8,128)}, f32[5,64,128]{2,1,0:T(8,128)S(1)}, u32[]{:S(2)}, u32[]{:S(2)}) collective-permute-start(f32[5,64,128]{2,1,0:T(8,128)} %get-tuple-element.17), channel_id=1, source_target_pairs={{0,8},{4,12},{8,0},{12,4},{1,9},{5,13},{9,1},{13,5},{2,10},{6,14},... | collective-permute-start | bytes 491528 | tf_op jit(solution)/shard_map/ppermute | solution.py:371
  40.9 1.4 %collective-permute-start.2 = (f32[5,64,128]{2,1,0:T(8,128)}, f32[5,64,128]{2,1,0:T(8,128)S(1)}, u32[]{:S(2)}, u32[]{:S(2)}) collective-permute-start(f32[5,64,128]{2,1,0:T(8,128)} %get-tuple-element.18), channel_id=1, source_target_pairs={{0,12},{4,0},{8,4},{12,8},{1,13},{5,1},{9,5},{13,9},{2,14},{6,2},{... | collective-permute-start | bytes 491528 | tf_op jit(solution)/shard_map/ppermute | solution.py:371
  42.3 3.4 %collective-permute-done.refs_1_ = f32[5,64,128]{2,1,0:T(8,128)S(1)} collective-permute-done((f32[5,64,128]{2,1,0:T(8,128)}, f32[5,64,128]{2,1,0:T(8,128)S(1)}, u32[]{:S(2)}, u32[]{:S(2)}) %collective-permute-start) | collective-permute-done | bytes 163872 | tf_op jit(solution)/shard_map/ppermute | solution.py:371
  45.7 0.0 copy-start
  45.7 6.2 %collective-permute-done.1.refs_2_ = f32[5,64,128]{2,1,0:T(8,128)S(1)} collective-permute-done((f32[5,64,128]{2,1,0:T(8,128)}, f32[5,64,128]{2,1,0:T(8,128)S(1)}, u32[]{:S(2)}, u32[]{:S(2)}) %collective-permute-start.1) | collective-permute-done | bytes 163872 | tf_op jit(solution)/shard_map/ppermute | solution.py:371
  51.9 0.0 copy-start.1
  51.9 0.0 collective-permute-done.2.refs_3_
  51.9 0.0 copy-start.2
  51.9 0.0 copy-done
  51.9 0.6 copy-done.1
  52.6 0.1 copy-done.2
  52.6 0.0 copy-start.6
  52.6 2.7 %chain.1 = (f32[5,32,128]{2,1,0:T(8,128)}, f32[5,32,128]{2,1,0:T(8,128)}, f32[5,32,128]{2,1,0:T(8,128)}, f32[5,32,128]{2,1,0:T(8,128)}, f32[320,64]{1,0:T(8,128)}) custom-call(f32[5,64,128]{2,1,0:T(8,128)} %get-tuple-element.15.refs_0_, f32[5,64,128]{2,1,0:T(8,128)} %copy-done, f32[5,64,128]{2,1,0:T(8,128)} %copy-done.1, f32[5,64,128]{2,1,0:T(8,128)} %copy-done.2), custom_call_target="tpu_custom_call" | custom-call | tf_op jit(solution)/shard_map/chain/pallas_call | solution.py:293
  55.4 3.9 %collective-permute-start.3 = (f32[5,32,128]{2,1,0:T(8,128)}, f32[5,32,128]{2,1,0:T(8,128)S(1)}, u32[]{:S(2)}, u32[]{:S(2)}) collective-permute-start(f32[5,32,128]{2,1,0:T(8,128)} %get-tuple-element.20), channel_id=1, source_target_pairs={{0,4},{4,8},{8,12},{12,0},{1,5},{5,9},{9,13},{13,1},{2,6},{6,10},{... | collective-permute-start | bytes 245768 | tf_op jit(solution)/shard_map/ppermute | solution.py:371
  59.3 1.7 %collective-permute-start.4 = (f32[5,32,128]{2,1,0:T(8,128)}, f32[5,32,128]{2,1,0:T(8,128)S(1)}, u32[]{:S(2)}, u32[]{:S(2)}) collective-permute-start(f32[5,32,128]{2,1,0:T(8,128)} %get-tuple-element.21), channel_id=1, source_target_pairs={{0,8},{4,12},{8,0},{12,4},{1,9},{5,13},{9,1},{13,5},{2,10},{6,14},... | collective-permute-start | bytes 245768 | tf_op jit(solution)/shard_map/ppermute | solution.py:371
  61.0 0.7 collective-permute-start.5
  61.7 0.0 copy-done.6
  61.7 0.6 reshape.11.refs_8_
  62.3 1.7 %copy.10 = f32[1,320,64]{1,2,0:T(8,128)} copy(f32[1,320,64]{2,1,0:T(8,128)} %bitcast.15) | data formatting | bytes 163840
  63.9 0.0 collective-permute-done.3.refs_1_
  63.9 0.0 copy-start.3
  63.9 2.8 %collective-permute-done.4.refs_2_ = f32[5,32,128]{2,1,0:T(8,128)S(1)} collective-permute-done((f32[5,32,128]{2,1,0:T(8,128)}, f32[5,32,128]{2,1,0:T(8,128)S(1)}, u32[]{:S(2)}, u32[]{:S(2)}) %collective-permute-start.4) | collective-permute-done | bytes 81952 | tf_op jit(solution)/shard_map/ppermute | solution.py:371
  66.7 0.0 copy-start.4
  66.7 0.4 collective-permute-done.5.refs_3_
  67.1 0.0 copy-start.5
  67.1 0.0 copy-done.3
  67.1 0.2 copy-done.4
  67.3 0.4 copy-done.5
  67.8 5.1 %finish.1 = bf16[128,1280]{1,0:T(8,128)(2,1)} custom-call(f32[5,32,128]{2,1,0:T(8,128)} %get-tuple-element.19.refs_0_, f32[5,32,128]{2,1,0:T(8,128)} %copy-done.3, f32[5,32,128]{2,1,0:T(8,128)} %copy-done.4, f32[5,32,128]{2,1,0:T(8,128)} %copy-done.5, bf16[1280,128]{1,0:T(8,128)(2,1)} %get-tuple-element.23.refs_4_, ...), custom_call_target="tpu_custom_call" | custom-call | tf_op jit(solution)/shard_map/finish/pallas_call | solution.py:359
Async XLA Ops:
  35.3 10.5 %collective-permute-start = (f32[5,64,128]{2,1,0:T(8,128)}, f32[5,64,128]{2,1,0:T(8,128)S(1)}, u32[]{:S(2)}, u32[]{:S(2)}) collective-permute-start(f32[5,64,128]{2,1,0:T(8,128)} %get-tuple-element.16), channel_id=1, source_target_pairs={{0,4},{4,8},{8,12},{12,0},{1,5},{5,9},{9,13},{13,1},{2,6},{6,10},{... | collective-permute-start | bytes 491528 | tf_op jit(solution)/shard_map/ppermute | solution.py:371
  38.4 13.5 %collective-permute-start.1 = (f32[5,64,128]{2,1,0:T(8,128)}, f32[5,64,128]{2,1,0:T(8,128)S(1)}, u32[]{:S(2)}, u32[]{:S(2)}) collective-permute-start(f32[5,64,128]{2,1,0:T(8,128)} %get-tuple-element.17), channel_id=1, source_target_pairs={{0,8},{4,12},{8,0},{12,4},{1,9},{5,13},{9,1},{13,5},{2,10},{6,14},... | collective-permute-start | bytes 491528 | tf_op jit(solution)/shard_map/ppermute | solution.py:371
  40.9 11.0 %collective-permute-start.2 = (f32[5,64,128]{2,1,0:T(8,128)}, f32[5,64,128]{2,1,0:T(8,128)S(1)}, u32[]{:S(2)}, u32[]{:S(2)}) collective-permute-start(f32[5,64,128]{2,1,0:T(8,128)} %get-tuple-element.18), channel_id=1, source_target_pairs={{0,12},{4,0},{8,4},{12,8},{1,13},{5,1},{9,5},{13,9},{2,14},{6,2},{... | collective-permute-start | bytes 491528 | tf_op jit(solution)/shard_map/ppermute | solution.py:371
  45.7 6.2 %copy-start = (f32[5,64,128]{2,1,0:T(8,128)}, f32[5,64,128]{2,1,0:T(8,128)S(1)}, u32[]{:S(2)}) copy-start(f32[5,64,128]{2,1,0:T(8,128)S(1)} %collective-permute-done.refs_1_) | copy-start | bytes 491524
  51.9 0.7 copy-start.1
  51.9 0.7 copy-start.2
  52.6 9.0 %copy-start.6 = (f32[1280]{0:T(1024)S(1)}, f32[1280]{0:T(1024)}, u32[]{:S(2)}) copy-start(f32[1280]{0:T(1024)} %param.15) | copy-start | bytes 15364
  55.4 8.6 %collective-permute-start.3 = (f32[5,32,128]{2,1,0:T(8,128)}, f32[5,32,128]{2,1,0:T(8,128)S(1)}, u32[]{:S(2)}, u32[]{:S(2)}) collective-permute-start(f32[5,32,128]{2,1,0:T(8,128)} %get-tuple-element.20), channel_id=1, source_target_pairs={{0,4},{4,8},{8,12},{12,0},{1,5},{5,9},{9,13},{13,1},{2,6},{6,10},{... | collective-permute-start | bytes 245768 | tf_op jit(solution)/shard_map/ppermute | solution.py:371
  59.3 7.4 %collective-permute-start.4 = (f32[5,32,128]{2,1,0:T(8,128)}, f32[5,32,128]{2,1,0:T(8,128)S(1)}, u32[]{:S(2)}, u32[]{:S(2)}) collective-permute-start(f32[5,32,128]{2,1,0:T(8,128)} %get-tuple-element.21), channel_id=1, source_target_pairs={{0,8},{4,12},{8,0},{12,4},{1,9},{5,13},{9,1},{13,5},{2,10},{6,14},... | collective-permute-start | bytes 245768 | tf_op jit(solution)/shard_map/ppermute | solution.py:371
  61.0 6.1 %collective-permute-start.5 = (f32[5,32,128]{2,1,0:T(8,128)}, f32[5,32,128]{2,1,0:T(8,128)S(1)}, u32[]{:S(2)}, u32[]{:S(2)}) collective-permute-start(f32[5,32,128]{2,1,0:T(8,128)} %get-tuple-element.22), channel_id=1, source_target_pairs={{0,12},{4,0},{8,4},{12,8},{1,13},{5,1},{9,5},{13,9},{2,14},{6,2},{... | collective-permute-start | bytes 245768 | tf_op jit(solution)/shard_map/ppermute | solution.py:371
  63.9 3.2 %copy-start.3 = (f32[5,32,128]{2,1,0:T(8,128)}, f32[5,32,128]{2,1,0:T(8,128)S(1)}, u32[]{:S(2)}) copy-start(f32[5,32,128]{2,1,0:T(8,128)S(1)} %collective-permute-done.3.refs_1_) | copy-start | bytes 245764
  66.7 0.6 copy-start.4
  67.1 0.6 copy-start.5

commit v2 on v1

v2 whole, which is shorter than its diff:
```python
import functools

import jax
import jax.numpy as jnp
from jax import lax
from jax.experimental import pallas as pl
from jax.experimental.pallas import tpu as pltpu
from jax.sharding import PartitionSpec as P

GROUP_DIMENSION = 64
PAIR = 2 * GROUP_DIMENSION
KEY_EPS = 1e-05
NORM_EPS = 0.00064
STEP_PAIRS = 5

F32 = jnp.float32
BF16 = jnp.bfloat16


def mm(left, right):
    return jnp.dot(left, right, preferred_element_type=F32)


def split(x):
    high = x.astype(BF16)
    return high, (x - high.astype(F32)).astype(BF16)


def side(*parts):
    return jnp.concatenate(parts, axis=1)


def stack(*parts):
    return jnp.concatenate(parts, axis=0)


def mm3(left, right):
    lh, ll = left
    rh, rl = right
    return mm(side(lh, ll), stack(rh, rh)) + mm(lh, rl)


def iota(shape, axis):
    return lax.broadcasted_iota(jnp.int32, shape, axis)


def group_ones():
    same = (iota((PAIR, PAIR), 0) // GROUP_DIMENSION) == (
        iota((PAIR, PAIR), 1) // GROUP_DIMENSION
    )
    ones = same.astype(F32).astype(BF16)
    return stack(ones, ones)


def group_sums(x, ones):
    parts = []
    for p in range(x.shape[1] // PAIR):
        high, low = split(x[:, p * PAIR : (p + 1) * PAIR])
        parts.append(mm(side(high, low), ones))
    return side(*parts)


def block_diagonal(x):
    top, bottom = x[:GROUP_DIMENSION], x[GROUP_DIMENSION:]
    none = jnp.zeros_like(top)
    return stack(side(top, none), side(none, bottom))


def product(left, right):
    rows = side(*right)
    full = mm(side(*left), stack(rows, rows))
    return full[:, :PAIR] + full[:, PAIR:]


def scores(late, away, keys, query):
    half = away[0].shape[0] // 2
    qh, ql = (block_diagonal(q) for q in query)
    early_rows = tuple(stack(a[:half], k[:half]) for a, k in zip(away, keys))
    late_rows = tuple(stack(a[half:], k[half:]) for a, k in zip(away, keys))
    early = mm3(early_rows, (qh, ql))
    later = mm3(late_rows, (qh * late, ql * late))
    return stack(early[:half], later[:half]), stack(early[half:], later[half:])


def late_columns(tokens):
    lane = iota((PAIR, 2 * tokens), 1) % tokens
    return (lane >= tokens // 2).astype(F32).astype(BF16)


def cumulative(log_step):
    tokens = log_step.shape[0]
    shape = (tokens, tokens)
    lower = (iota(shape, 0) >= iota(shape, 1)).astype(F32).astype(BF16)
    high, low = split(log_step)
    lowest = (log_step - high.astype(F32) - low.astype(F32)).astype(BF16)
    return mm(side(lower, lower), stack(high, low)) + mm(lower, lowest)


def key_side(fade_ref, removal_ref, rate_ref, key_ref, ones):
    half = fade_ref.shape[0] // 2
    log_step = -jnp.exp(fade_ref[...].astype(F32))
    cum = cumulative(log_step)
    middle = cum[half - 1 : half]
    removal = removal_ref[...].astype(F32)
    norm = group_sums(removal * removal, ones) * (1.0 / GROUP_DIMENSION)
    kappa = removal * lax.rsqrt(norm + KEY_EPS) * GROUP_DIMENSION ** (-0.5)
    inverse = jnp.exp(middle - cum)
    away = kappa * rate_ref[...].astype(F32) * inverse
    keys = key_ref[...].astype(F32) * inverse
    return log_step, cum, middle, kappa, away, keys


def range_kernel(
    owners, fade_ref, key_ref, value_ref, removal_ref, rate_ref, *rest
):
    send_refs = rest[:owners]
    solved_ref, held, sems = rest[owners:]
    step = pl.program_id(0)
    me = lax.axis_index("seq")
    tokens, width = fade_ref.shape
    pairs = width // PAIR
    per_owner = held.shape[1]
    d = GROUP_DIMENSION

    ones = group_ones()
    late = late_columns(tokens)
    strict = iota((tokens, tokens), 0) < iota((tokens, tokens), 1)
    log_step, cum, middle, kappa, away, keys = key_side(
        fade_ref, removal_ref, rate_ref, key_ref, ones
    )
    end = cum[tokens - 1 : tokens]
    before = cum - log_step
    to_end = jnp.exp(end - middle)
    gamma_end = jnp.exp(end)
    toward_mid = -kappa * jnp.exp(before - middle)
    toward_abs = -kappa * jnp.exp(before)
    value = value_ref[...].astype(F32)

    cuts = [slice(p * PAIR, (p + 1) * PAIR) for p in range(pairs)]
    solved, powers, twice = [], [], []
    for cut in cuts:
        mix_away, mix_keys = scores(
            late, split(away[:, cut]), split(keys[:, cut]), split(toward_mid[:, cut].T)
        )
        start = toward_abs[:, cut].T
        value_t = value[:, cut].T.astype(BF16)
        for i in range(2):
            lanes = slice(i * tokens, (i + 1) * tokens)
            rows = slice(i * d, (i + 1) * d)
            values = side(value_t[rows], value_t[rows])
            mixed = split(jnp.where(strict, mix_keys[:, lanes], 0.0))
            solved.append(stack(start[rows], mm(values, stack(*mixed))))
            powers.append(jnp.where(strict, mix_away[:, lanes], 0.0))
            twice.append(values)

    for h in range(2 * pairs):
        ps = split(powers[h])
        out = product(tuple(stack(w, q) for w, q in zip(split(solved[h]), ps)), ps)
        solved[h] = solved[h] + out[:tokens]
        powers[h] = out[tokens:].astype(BF16)
    both = [side(*solved[2 * p : 2 * p + 2]) for p in range(pairs)]
    none = jnp.zeros((tokens, tokens), BF16)
    reach = 2
    while reach < tokens:
        for p in range(pairs):
            one, two = powers[2 * p : 2 * p + 2]
            factor = stack(side(one, none), side(none, two))
            left = both[p].astype(BF16)
            if reach * 2 < tokens:
                out = mm(stack(left, side(one, two)), factor)
                square = out[tokens:].astype(BF16)
                powers[2 * p] = square[:, :tokens]
                powers[2 * p + 1] = square[:, tokens:]
                both[p] = both[p] + out[:tokens]
            else:
                both[p] = both[p] + mm(left, factor)
        reach *= 2

    lane = iota((d, PAIR), 1)
    sub = iota((d, PAIR), 0)
    for p, cut in enumerate(cuts):
        away_end = split(away[:, cut] * to_end[:, cut])
        keys_end = split(keys[:, cut] * to_end[:, cut])
        for i in range(2):
            ws = split(both[p][:, i * tokens : (i + 1) * tokens])
            solved_ref[2 * p + i] = side(*ws)
            ended = product(ws, away_end)
            stay = jnp.where(lane == sub + i * d, gamma_end[:, cut], 0.0)
            state_map = ended[:d] + stay
            state_add = ended[d:] + mm(twice[2 * p + i], stack(*keys_end))
            if i == 0:
                state_add = pltpu.roll(state_add, d, 1)
            else:
                state_map = pltpu.roll(state_map, d, 1)
            head = (step * pairs + p) * 2 + i
            slot = lax.rem(head // per_owner - me % owners + owners, owners)
            held[slot, lax.rem(head, per_owner)] = jnp.where(
                lane < d, state_map, state_add
            )

    @pl.when(step == pl.num_programs(0) - 1)
    def _():
        copies = [
            pltpu.make_async_copy(held.at[k], send_refs[k], sems.at[k])
            for k in range(owners)
        ]
        for copy in copies:
            copy.start()
        for copy in copies:
            copy.wait()


def specs(tokens, features):
    width = STEP_PAIRS * PAIR
    natural = pl.BlockSpec((tokens, width), lambda g: (0, g))
    turned = pl.BlockSpec((width, tokens), lambda g: (g, 0))
    vector = pl.BlockSpec((1, width), lambda g: (0, g))
    solved = pl.BlockSpec((2 * STEP_PAIRS, tokens, 2 * tokens), lambda g: (g, 0, 0))
    return (features // width,), natural, turned, vector, solved


def range_pass(owners, fade, key, value, removal, rate):
    tokens, features = fade.shape
    heads = features // GROUP_DIMENSION
    grid, natural, _, _, solved = specs(tokens, features)
    block = (heads // owners, GROUP_DIMENSION, PAIR)
    out = pl.pallas_call(
        functools.partial(range_kernel, owners),
        grid=grid,
        in_specs=[natural] * 5,
        out_specs=[pl.BlockSpec(memory_space=pl.ANY)] * owners + [solved],
        out_shape=[jax.ShapeDtypeStruct(block, F32)] * owners
        + [jax.ShapeDtypeStruct((heads, tokens, 2 * tokens), BF16)],
        scratch_shapes=[
            pltpu.VMEM((owners,) + block, F32),
            pltpu.SemaphoreType.DMA((owners,)),
        ],
        name="range_pass",
    )(fade, key, value, removal, rate)
    return out[:owners], out[owners]


def read_kernel(
    reader_ref,
    fade_ref,
    key_ref,
    value_ref,
    removal_ref,
    rate_ref,
    extra_ref,
    solved_ref,
    lift_high_ref,
    lift_low_ref,
    within_ref,
    bonus_ref,
):
    tokens, width = fade_ref.shape
    d = GROUP_DIMENSION
    ones = group_ones()
    late = late_columns(tokens)
    seen = iota((tokens, tokens), 0) <= iota((tokens, tokens), 1)
    _, cum, middle, _, away, keys = key_side(
        fade_ref, removal_ref, rate_ref, key_ref, ones
    )
    reader = reader_ref[...].astype(F32)
    value = value_ref[...].astype(F32)
    bonus = group_sums(reader * key_ref[...].astype(F32) * extra_ref[...], ones)
    bonus_ref[...] = bonus * value
    reader_mid = reader * jnp.exp(cum - middle)
    reader_abs = reader * jnp.exp(cum)

    for p in range(width // PAIR):
        cut = slice(p * PAIR, (p + 1) * PAIR)
        read_away, read_keys = scores(
            late, split(away[:, cut]), split(keys[:, cut]), split(reader_mid[:, cut].T)
        )
        start = reader_abs[:, cut].T
        value_t = value[:, cut].T.astype(BF16)
        for i in range(2):
            lanes = slice(i * tokens, (i + 1) * tokens)
            rows = slice(i * d, (i + 1) * d)
            at = slice(p * PAIR + i * d, p * PAIR + (i + 1) * d)
            both = solved_ref[2 * p + i]
            solved = both[:, :tokens], both[:, tokens:]
            values = side(value_t[rows], value_t[rows])
            read = product(solved, split(jnp.where(seen, read_away[:, lanes], 0.0)))
            direct = split(jnp.where(seen, read_keys[:, lanes], 0.0))
            within_ref[at] = read[d:] + mm(values, stack(*direct))
            lift_high_ref[at], lift_low_ref[at] = split(start[rows] + read[:d])


def read_pass(reader, fade, key, value, removal, rate, extra, solved):
    tokens, features = reader.shape
    grid, natural, turned, vector, solved_spec = specs(tokens, features)
    return pl.pallas_call(
        read_kernel,
        grid=grid,
        in_specs=[natural] * 6 + [vector, solved_spec],
        out_specs=[turned, turned, turned, natural],
        out_shape=[
            jax.ShapeDtypeStruct((features, tokens), BF16),
            jax.ShapeDtypeStruct((features, tokens), BF16),
            jax.ShapeDtypeStruct((features, tokens), F32),
            jax.ShapeDtypeStruct((tokens, features), F32),
        ],
        name="read_pass",
    )(reader, fade, key, value, removal, rate, extra, solved)


def pack_rows(state):
    rows = state.shape[0] // 2
    return side(state[:rows], state[rows:])


def chain_kernel(owners, *refs):
    got_refs = refs[:owners]
    state_refs = refs[owners : 2 * owners]
    final_ref, ranges, states = refs[2 * owners :]
    me = lax.axis_index("seq")
    per_owner = got_refs[0].shape[0]
    for k in range(owners):
        ranges[lax.rem(me - k + owners, owners)] = got_refs[k][...]
    d = GROUP_DIMENSION
    current = []
    for q in range(per_owner):
        states[0, q] = jnp.zeros((d // 2, PAIR), F32)
        current.append(ranges[0, q][:, d:])
    for i in range(1, owners + 1):
        for q in range(per_owner):
            if i < owners:
                states[i, q] = pack_rows(current[q])
                both = ranges[i, q]
                maps = split(both)
                moved = mm3(split(current[q]), maps)[:, :d]
                current[q] = moved + both[:, d:]
            else:
                final_ref[q * d : (q + 1) * d, :] = current[q]
    for k in range(owners):
        state_refs[k][...] = states[lax.rem(me + k, owners)]


def chain(got):
    owners = len(got)
    per_owner = got[0].shape[0]
    block = (per_owner, GROUP_DIMENSION // 2, PAIR)
    rows = per_owner * GROUP_DIMENSION
    whole = pl.BlockSpec(memory_space=pltpu.VMEM)
    out = pl.pallas_call(
        functools.partial(chain_kernel, owners),
        in_specs=[whole] * owners,
        out_specs=[whole] * (owners + 1),
        out_shape=[jax.ShapeDtypeStruct(block, F32)] * owners
        + [jax.ShapeDtypeStruct((rows, GROUP_DIMENSION), F32)],
        scratch_shapes=[
            pltpu.VMEM((owners,) + got[0].shape, F32),
            pltpu.VMEM((owners,) + block, F32),
        ],
        name="chain",
    )(*got)
    return out[:owners], out[owners]


def finish_kernel(owners, *refs):
    state_refs = refs[:owners]
    lift_high_ref, lift_low_ref, within_ref, bonus_ref, gain_ref = refs[
        owners : owners + 5
    ]
    out_ref, states = refs[owners + 5 :]
    step = pl.program_id(0)
    me = lax.axis_index("seq")
    per_owner = state_refs[0].shape[0]
    width = out_ref.shape[1]
    d = GROUP_DIMENSION

    @pl.when(step == 0)
    def _():
        for k in range(owners):
            states[lax.rem(me % owners - k + owners, owners)] = state_refs[k][...]

    lane = iota((d // 2, PAIR), 1)
    for p in range(width // PAIR):
        normed = []
        for i in range(2):
            head = (step * (width // PAIR) + p) * 2 + i
            packed = states[head // per_owner, lax.rem(head, per_owner)]
            state = split(
                stack(
                    jnp.where(lane < d, packed, 0.0),
                    jnp.where(lane >= d, packed, 0.0),
                )
            )
            at = slice(p * PAIR + i * d, p * PAIR + (i + 1) * d)
            high, low = lift_high_ref[at], lift_low_ref[at]
            result = within_ref[at] + mm3(
                state, (stack(high, high), stack(low, low))
            )
            average = jnp.mean(result, axis=0, keepdims=True)
            centered = result - average
            spread = jnp.mean(centered * centered, axis=0, keepdims=True)
            normed.append(centered * lax.rsqrt(spread + NORM_EPS))
        cut = slice(p * PAIR, (p + 1) * PAIR)
        turned = stack(*normed).T
        out_ref[:, cut] = (turned * gain_ref[:, cut] + bonus_ref[:, cut]).astype(BF16)


def finish(states, lift_high, lift_low, within, bonus, gain):
    owners = len(states)
    tokens, features = bonus.shape
    grid, natural, turned, vector, _ = specs(tokens, features)
    whole = pl.BlockSpec(memory_space=pltpu.VMEM)
    return pl.pallas_call(
        functools.partial(finish_kernel, owners),
        grid=grid,
        in_specs=[whole] * owners + [turned, turned, turned, natural, vector],
        out_specs=natural,
        out_shape=jax.ShapeDtypeStruct((tokens, features), BF16),
        scratch_shapes=[pltpu.VMEM((owners,) + states[0].shape, F32)],
        name="finish",
    )(*states, lift_high, lift_low, within, bonus, gain)


def shifted(value, by, members):
    return lax.ppermute(value, "seq", [(i, (i + by) % members) for i in range(members)])


def relay_states(both, members):
    d = GROUP_DIMENSION
    local_map, local_add = both[:, :, :d], both[:, :, d:]

    def relay(_, carried):
        pairs = [(i, i + 1) for i in range(members - 1)]
        incoming = lax.ppermute(carried[1], "seq", pairs)
        moved = jnp.einsum(
            "hvk,hkj->hvj", incoming, local_map, precision=lax.Precision.HIGHEST
        )
        return (incoming, moved + local_add)

    first = (jnp.zeros_like(local_add), local_add)
    incoming, leaving = lax.fori_loop(0, members - 1, relay, first)
    here = lax.axis_index("seq")
    closing = lax.psum(jnp.where(here == members - 1, leaving, 0.0), "seq")
    closing = closing.reshape(-1, d)
    rows = closing.shape[0] // members
    final = lax.dynamic_slice_in_dim(closing, here * rows, rows, 0)
    packed = jnp.concatenate([incoming[:, : d // 2], incoming[:, d // 2 :]], axis=2)
    return packed, final


def on_device(reader, fade, key, value, removal, rate, extra, gain):
    members = lax.axis_size("seq")
    features = reader.shape[2]
    heads = features // GROUP_DIMENSION
    owners = members if heads % members == 0 else 1
    keyed = (fade[0], key[0], value[0], removal[0], rate[0])
    sends, solved = range_pass(owners, *keyed)
    parts = read_pass(reader[0], *keyed, extra.reshape(1, features), solved)
    if owners > 1:
        got = [sends[0]] + [shifted(sends[k], k, members) for k in range(1, owners)]
        got, parts = lax.optimization_barrier((got, parts))
        states, final = chain(got)
        states = [states[0]] + [
            shifted(states[k], k, members) for k in range(1, owners)
        ]
    else:
        packed, final = relay_states(sends[0], members)
        states = [packed]
    blended = finish(states, *parts, gain.reshape(1, features))
    return (blended[None], final[None])


def solution(mesh):
    tokens = P(("groups", "dp"), "seq", None)
    return jax.shard_map(
        on_device,
        mesh=mesh,
        in_specs=(tokens,) * 6 + (P(), P()),
        out_specs=(tokens, tokens),
        check_vma=False,
    )
```

time: 73.2 us -> 47 us (0.64)
  Pallas kernels: 41.2 us -> 23.1 us
  waiting for transfers between devices: 12.8 us -> 5.45 us
    pallas_call x2 -> x3, Pallas kernels: 38.4 us -> 20.4 us  [the longest x1 10.5 us: range_pass(): pl.pallas_call(functools.partial(range_kernel, owners), grid=grid, in_spe...]
    ppermute x6, waiting for transfers between devices: 12.8 us -> 5.45 us  [shifted(): lax.ppermute(value, 'seq', [(i, (i + by) % members) for i in range(member...]
    unnamed x15 -> x17, local copies, waits for them, and re-layouts: 3.03 us -> 3.07 us
  transfers between devices with their start and end apart: 6 -> 6, of which waited for: 4 -> 3; matrix products, arithmetic and copies ran while one was open for 3% -> 6% of each run, Pallas kernels for 0% -> 14%
where the time goes in v2:
time: 47 us; the launch traced here: 46.8 us
  Pallas kernels  23.1 us (49%)
  starting transfers between devices  13.3 us (28%)
  waiting for transfers between devices  5.45 us (12%)
  local copies, waits for them, and re-layouts  4.26 us (9%)
  between operations  0.68 us (1%)
    ppermute x6, starting transfers between devices, shifted(): lax.ppermute(value, 'seq', [(i, (i + by) % members) for i in range(member...  13.3 us
    pallas_call x1, Pallas kernels, range_pass(): pl.pallas_call(functools.partial(range_kernel, owners), grid=grid, in_spe...  10.5 us
    pallas_call x1, Pallas kernels, read_pass(): pl.pallas_call(read_kernel, grid=grid, in_specs=[natural] * 6 + [vector,...  6.73 us
    ppermute x6, waiting for transfers between devices, shifted(): lax.ppermute(value, 'seq', [(i, (i + by) % members) for i in range(member...  5.45 us
    pallas_call x1, Pallas kernels, finish(): pl.pallas_call(functools.partial(finish_kernel, owners), grid=grid, in_sp...  3.13 us
    unnamed x17, local copies, waits for them, and re-layouts  3.07 us
    pallas_call x1, Pallas kernels, chain(): pl.pallas_call(functools.partial(chain_kernel, owners), in_specs=[whole]...  2.7 us
  transfers between devices with their start and end apart: 6, of which 3 were waited for; matrix products, arithmetic and copies ran while one was open for 6% of the time, Pallas kernels for 14%

profile of v2, /device:TPU:0, one launch (start us, length us, event | category | flops | bytes accessed | tf_op | source)
XLA Modules:
  0.0 46.8 jit_solution(408546214853573031)
XLA Ops:
  0.6 0.0 copy-start.6
  0.6 10.5 %range_pass.1 = (f32[5,64,128]{2,1,0:T(8,128)}, f32[5,64,128]{2,1,0:T(8,128)}, f32[5,64,128]{2,1,0:T(8,128)}, f32[5,64,128]{2,1,0:T(8,128)}, bf16[20,128,256]{2,1,0:T(8,128)(2,1)}) custom-call(bf16[128,1280]{1,0:T(8,128)(2,1)} %bitcast.8, bf16[128,1280]{1,0:T(8,128)(2,1)} %bitcast.10, bf16[128,1280]{1,0:T(8,128)(2,1)} %bitcast.12, ...), custom_call_target="tpu_custom_call" | custom-call | tf_op jit(solution)/shard_map/range_pass/pallas_call | solution.py:227
  11.2 3.1 %collective-permute-start = (f32[5,64,128]{2,1,0:T(8,128)}, f32[5,64,128]{2,1,0:T(8,128)S(1)}, u32[]{:S(2)}, u32[]{:S(2)}) collective-permute-start(f32[5,64,128]{2,1,0:T(8,128)} %get-tuple-element.25), channel_id=1, source_target_pairs={{0,4},{4,8},{8,12},{12,0},{1,5},{5,9},{9,13},{13,1},{2,6},{6,10},{... | collective-permute-start | bytes 491528 | tf_op jit(solution)/shard_map/ppermute | solution.py:423
  14.3 2.6 %collective-permute-start.1 = (f32[5,64,128]{2,1,0:T(8,128)}, f32[5,64,128]{2,1,0:T(8,128)S(1)}, u32[]{:S(2)}, u32[]{:S(2)}) collective-permute-start(f32[5,64,128]{2,1,0:T(8,128)} %get-tuple-element.26), channel_id=1, source_target_pairs={{0,8},{4,12},{8,0},{12,4},{1,9},{5,13},{9,1},{13,5},{2,10},{6,14},... | collective-permute-start | bytes 491528 | tf_op jit(solution)/shard_map/ppermute | solution.py:423
  16.9 1.3 %collective-permute-start.2 = (f32[5,64,128]{2,1,0:T(8,128)}, f32[5,64,128]{2,1,0:T(8,128)S(1)}, u32[]{:S(2)}, u32[]{:S(2)}) collective-permute-start(f32[5,64,128]{2,1,0:T(8,128)} %get-tuple-element.27), channel_id=1, source_target_pairs={{0,12},{4,0},{8,4},{12,8},{1,13},{5,1},{9,5},{13,9},{2,14},{6,2},{... | collective-permute-start | bytes 491528 | tf_op jit(solution)/shard_map/ppermute | solution.py:423
  18.2 0.0 copy-done.6
  18.2 0.6 %reshape.10.extra_ref = f32[1,1280]{1,0:T(1,128)} reshape(f32[1280]{0:T(1024)S(1)} %copy-done.6) | data formatting | bytes 10240 | tf_op jit(solution)/shard_map/reshape | solution.py:456
  18.8 0.0 copy-start.7
  18.8 6.7 %read_pass.1 = (bf16[1280,128]{1,0:T(8,128)(2,1)}, bf16[1280,128]{1,0:T(8,128)(2,1)}, f32[1280,128]{1,0:T(8,128)}, f32[128,1280]{1,0:T(8,128)}) custom-call(bf16[128,1280]{1,0:T(8,128)(2,1)} %bitcast.18, bf16[128,1280]{1,0:T(8,128)(2,1)} %bitcast.9, bf16[128,1280]{1,0:T(8,128)(2,1)} %bitcast.11, bf16[128,1280]{1,0:T(8,128)(2,1)} %bitcast.13, ...), custom_call_target="tpu_custom_call" | custom-call | tf_op jit(solution)/shard_map/read_pass/pallas_call | solution.py:295
  25.6 0.0 collective-permute-done.refs_1_
  25.6 0.0 copy-start
  25.6 2.3 %collective-permute-done.1.refs_2_ = f32[5,64,128]{2,1,0:T(8,128)S(1)} collective-permute-done((f32[5,64,128]{2,1,0:T(8,128)}, f32[5,64,128]{2,1,0:T(8,128)S(1)}, u32[]{:S(2)}, u32[]{:S(2)}) %collective-permute-start.1) | collective-permute-done | bytes 163872 | tf_op jit(solution)/shard_map/ppermute | solution.py:423
  27.8 0.0 copy-start.1
  27.8 0.0 collective-permute-done.2.refs_3_
  27.8 0.0 copy-start.2
  27.8 0.0 copy-done
  27.9 0.7 %copy-done.1 = f32[5,64,128]{2,1,0:T(8,128)} copy-done((f32[5,64,128]{2,1,0:T(8,128)}, f32[5,64,128]{2,1,0:T(8,128)S(1)}, u32[]{:S(2)}) %copy-start.1) | copy-done | bytes 163864
  28.5 0.1 copy-done.2
  28.6 2.7 %chain.1 = (f32[5,32,128]{2,1,0:T(8,128)}, f32[5,32,128]{2,1,0:T(8,128)}, f32[5,32,128]{2,1,0:T(8,128)}, f32[5,32,128]{2,1,0:T(8,128)}, f32[320,64]{1,0:T(8,128)}) custom-call(f32[5,64,128]{2,1,0:T(8,128)} %get-tuple-element.33.refs_0_, f32[5,64,128]{2,1,0:T(8,128)} %copy-done, f32[5,64,128]{2,1,0:T(8,128)} %copy-done.1, f32[5,64,128]{2,1,0:T(8,128)} %copy-done.2), custom_call_target="tpu_custom_call" | custom-call | tf_op jit(solution)/shard_map/chain/pallas_call | solution.py:348
  31.3 3.9 %collective-permute-start.3 = (f32[5,32,128]{2,1,0:T(8,128)}, f32[5,32,128]{2,1,0:T(8,128)S(1)}, u32[]{:S(2)}, u32[]{:S(2)}) collective-permute-start(f32[5,32,128]{2,1,0:T(8,128)} %get-tuple-element.38), channel_id=1, source_target_pairs={{0,4},{4,8},{8,12},{12,0},{1,5},{5,9},{9,13},{13,1},{2,6},{6,10},{... | collective-permute-start | bytes 245768 | tf_op jit(solution)/shard_map/ppermute | solution.py:423
  35.2 1.7 %collective-permute-start.4 = (f32[5,32,128]{2,1,0:T(8,128)}, f32[5,32,128]{2,1,0:T(8,128)S(1)}, u32[]{:S(2)}, u32[]{:S(2)}) collective-permute-start(f32[5,32,128]{2,1,0:T(8,128)} %get-tuple-element.39), channel_id=1, source_target_pairs={{0,8},{4,12},{8,0},{12,4},{1,9},{5,13},{9,1},{13,5},{2,10},{6,14},... | collective-permute-start | bytes 245768 | tf_op jit(solution)/shard_map/ppermute | solution.py:423
  36.9 0.6 %collective-permute-start.5 = (f32[5,32,128]{2,1,0:T(8,128)}, f32[5,32,128]{2,1,0:T(8,128)S(1)}, u32[]{:S(2)}, u32[]{:S(2)}) collective-permute-start(f32[5,32,128]{2,1,0:T(8,128)} %get-tuple-element.40), channel_id=1, source_target_pairs={{0,12},{4,0},{8,4},{12,8},{1,13},{5,1},{9,5},{13,9},{2,14},{6,2},{... | collective-permute-start | bytes 245768 | tf_op jit(solution)/shard_map/ppermute | solution.py:423
  37.6 0.0 copy-done.7
  37.6 0.6 %reshape.11.refs_8_ = f32[1,1280]{1,0:T(1,128)} reshape(f32[1280]{0:T(1024)S(1)} %copy-done.7) | data formatting | bytes 10240 | tf_op jit(solution)/shard_map/reshape | solution.py:467
  38.2 1.7 %copy.10 = f32[1,320,64]{1,2,0:T(8,128)} copy(f32[1,320,64]{2,1,0:T(8,128)} %bitcast.20) | data formatting | bytes 163840
  39.8 0.0 collective-permute-done.3.refs_1_
  39.8 0.0 copy-start.3
  39.8 2.8 %collective-permute-done.4.refs_2_ = f32[5,32,128]{2,1,0:T(8,128)S(1)} collective-permute-done((f32[5,32,128]{2,1,0:T(8,128)}, f32[5,32,128]{2,1,0:T(8,128)S(1)}, u32[]{:S(2)}, u32[]{:S(2)}) %collective-permute-start.4) | collective-permute-done | bytes 81952 | tf_op jit(solution)/shard_map/ppermute | solution.py:423
  42.6 0.0 copy-start.4
  42.6 0.4 collective-permute-done.5.refs_3_
  43.0 0.0 copy-start.5
  43.0 0.0 copy-done.3
  43.0 0.2 copy-done.4
  43.3 0.4 copy-done.5
  43.7 3.1 %finish.1 = bf16[128,1280]{1,0:T(8,128)(2,1)} custom-call(f32[5,32,128]{2,1,0:T(8,128)} %get-tuple-element.37.refs_0_, f32[5,32,128]{2,1,0:T(8,128)} %copy-done.3, f32[5,32,128]{2,1,0:T(8,128)} %copy-done.4, f32[5,32,128]{2,1,0:T(8,128)} %copy-done.5, bf16[1280,128]{1,0:T(8,128)(2,1)} %get-tuple-element.41.refs_4_, ...), custom_call_target="tpu_custom_call" | custom-call | tf_op jit(solution)/shard_map/finish/pallas_call | solution.py:411
Async XLA Ops:
  0.6 17.6 %copy-start.6 = (f32[1280]{0:T(1024)S(1)}, f32[1280]{0:T(1024)}, u32[]{:S(2)}) copy-start(f32[1280]{0:T(1024)} %param.14) | copy-start | bytes 15364
  11.2 14.4 %collective-permute-start = (f32[5,64,128]{2,1,0:T(8,128)}, f32[5,64,128]{2,1,0:T(8,128)S(1)}, u32[]{:S(2)}, u32[]{:S(2)}) collective-permute-start(f32[5,64,128]{2,1,0:T(8,128)} %get-tuple-element.25), channel_id=1, source_target_pairs={{0,4},{4,8},{8,12},{12,0},{1,5},{5,9},{9,13},{13,1},{2,6},{6,10},{... | collective-permute-start | bytes 491528 | tf_op jit(solution)/shard_map/ppermute | solution.py:423
  14.3 13.5 %collective-permute-start.1 = (f32[5,64,128]{2,1,0:T(8,128)}, f32[5,64,128]{2,1,0:T(8,128)S(1)}, u32[]{:S(2)}, u32[]{:S(2)}) collective-permute-start(f32[5,64,128]{2,1,0:T(8,128)} %get-tuple-element.26), channel_id=1, source_target_pairs={{0,8},{4,12},{8,0},{12,4},{1,9},{5,13},{9,1},{13,5},{2,10},{6,14},... | collective-permute-start | bytes 491528 | tf_op jit(solution)/shard_map/ppermute | solution.py:423
  16.9 11.0 %collective-permute-start.2 = (f32[5,64,128]{2,1,0:T(8,128)}, f32[5,64,128]{2,1,0:T(8,128)S(1)}, u32[]{:S(2)}, u32[]{:S(2)}) collective-permute-start(f32[5,64,128]{2,1,0:T(8,128)} %get-tuple-element.27), channel_id=1, source_target_pairs={{0,12},{4,0},{8,4},{12,8},{1,13},{5,1},{9,5},{13,9},{2,14},{6,2},{... | collective-permute-start | bytes 491528 | tf_op jit(solution)/shard_map/ppermute | solution.py:423
  18.8 18.7 %copy-start.7 = (f32[1280]{0:T(1024)S(1)}, f32[1280]{0:T(1024)}, u32[]{:S(2)}) copy-start(f32[1280]{0:T(1024)} %param.15) | copy-start | bytes 15364
  25.6 2.3 %copy-start = (f32[5,64,128]{2,1,0:T(8,128)}, f32[5,64,128]{2,1,0:T(8,128)S(1)}, u32[]{:S(2)}) copy-start(f32[5,64,128]{2,1,0:T(8,128)S(1)} %collective-permute-done.refs_1_) | copy-start | bytes 491524
  27.8 0.7 %copy-start.1 = (f32[5,64,128]{2,1,0:T(8,128)}, f32[5,64,128]{2,1,0:T(8,128)S(1)}, u32[]{:S(2)}) copy-start(f32[5,64,128]{2,1,0:T(8,128)S(1)} %collective-permute-done.1.refs_2_) | copy-start | bytes 491524
  27.8 0.8 %copy-start.2 = (f32[5,64,128]{2,1,0:T(8,128)}, f32[5,64,128]{2,1,0:T(8,128)S(1)}, u32[]{:S(2)}) copy-start(f32[5,64,128]{2,1,0:T(8,128)S(1)} %collective-permute-done.2.refs_3_) | copy-start | bytes 491524
  31.3 8.5 %collective-permute-start.3 = (f32[5,32,128]{2,1,0:T(8,128)}, f32[5,32,128]{2,1,0:T(8,128)S(1)}, u32[]{:S(2)}, u32[]{:S(2)}) collective-permute-start(f32[5,32,128]{2,1,0:T(8,128)} %get-tuple-element.38), channel_id=1, source_target_pairs={{0,4},{4,8},{8,12},{12,0},{1,5},{5,9},{9,13},{13,1},{2,6},{6,10},{... | collective-permute-start | bytes 245768 | tf_op jit(solution)/shard_map/ppermute | solution.py:423
  35.2 7.4 %collective-permute-start.4 = (f32[5,32,128]{2,1,0:T(8,128)}, f32[5,32,128]{2,1,0:T(8,128)S(1)}, u32[]{:S(2)}, u32[]{:S(2)}) collective-permute-start(f32[5,32,128]{2,1,0:T(8,128)} %get-tuple-element.39), channel_id=1, source_target_pairs={{0,8},{4,12},{8,0},{12,4},{1,9},{5,13},{9,1},{13,5},{2,10},{6,14},... | collective-permute-start | bytes 245768 | tf_op jit(solution)/shard_map/ppermute | solution.py:423
  36.9 6.1 %collective-permute-start.5 = (f32[5,32,128]{2,1,0:T(8,128)}, f32[5,32,128]{2,1,0:T(8,128)S(1)}, u32[]{:S(2)}, u32[]{:S(2)}) collective-permute-start(f32[5,32,128]{2,1,0:T(8,128)} %get-tuple-element.40), channel_id=1, source_target_pairs={{0,12},{4,0},{8,4},{12,8},{1,13},{5,1},{9,5},{13,9},{2,14},{6,2},{... | collective-permute-start | bytes 245768 | tf_op jit(solution)/shard_map/ppermute | solution.py:423
  39.8 3.2 %copy-start.3 = (f32[5,32,128]{2,1,0:T(8,128)}, f32[5,32,128]{2,1,0:T(8,128)S(1)}, u32[]{:S(2)}) copy-start(f32[5,32,128]{2,1,0:T(8,128)S(1)} %collective-permute-done.3.refs_1_) | copy-start | bytes 245764
  42.6 0.6 %copy-start.4 = (f32[5,32,128]{2,1,0:T(8,128)}, f32[5,32,128]{2,1,0:T(8,128)S(1)}, u32[]{:S(2)}) copy-start(f32[5,32,128]{2,1,0:T(8,128)S(1)} %collective-permute-done.4.refs_2_) | copy-start | bytes 245764
  43.0 0.6 %copy-start.5 = (f32[5,32,128]{2,1,0:T(8,128)}, f32[5,32,128]{2,1,0:T(8,128)S(1)}, u32[]{:S(2)}) copy-start(f32[5,32,128]{2,1,0:T(8,128)S(1)} %collective-permute-done.5.refs_3_) | copy-start | bytes 245764

commit v3 on v2

v3 whole, which is shorter than its diff:
```python
import functools

import jax
import jax.numpy as jnp
from jax import lax
from jax.experimental import pallas as pl
from jax.experimental.pallas import tpu as pltpu
from jax.sharding import PartitionSpec as P

GROUP_DIMENSION = 64
PAIR = 2 * GROUP_DIMENSION
KEY_EPS = 1e-05
NORM_EPS = 0.00064

F32 = jnp.float32
BF16 = jnp.bfloat16


def mm(left, right):
    return jnp.dot(left, right, preferred_element_type=F32)


def split(x):
    high = x.astype(BF16)
    return high, (x - high.astype(F32)).astype(BF16)


def side(*parts):
    return jnp.concatenate(parts, axis=1)


def stack(*parts):
    return jnp.concatenate(parts, axis=0)


def mm3(left, right):
    lh, ll = left
    rh, rl = right
    return mm(side(lh, ll), stack(rh, rh)) + mm(lh, rl)


def iota(shape, axis):
    return lax.broadcasted_iota(jnp.int32, shape, axis)


def group_ones():
    same = (iota((PAIR, PAIR), 0) // GROUP_DIMENSION) == (
        iota((PAIR, PAIR), 1) // GROUP_DIMENSION
    )
    ones = same.astype(F32).astype(BF16)
    return stack(ones, ones)


def group_sums(x, ones):
    parts = []
    for p in range(x.shape[1] // PAIR):
        high, low = split(x[:, p * PAIR : (p + 1) * PAIR])
        parts.append(mm(side(high, low), ones))
    return side(*parts)


def block_diagonal(x):
    top, bottom = x[:GROUP_DIMENSION], x[GROUP_DIMENSION:]
    none = jnp.zeros_like(top)
    return stack(side(top, none), side(none, bottom))


def folded(left, right):
    full = mm(left, right)
    return full[:, :PAIR] + full[:, PAIR:]


def lane_blocks(x, low, high):
    parts = []
    for i in range(2):
        one = x[:, i * PAIR : (i + 1) * PAIR]
        none = jnp.zeros_like(one)
        for mask in (low, high):
            kept = one * mask
            parts.append(side(kept, none) if i == 0 else side(none, kept))
    return stack(*parts)


def scores(late, away, keys, query, terms):
    half = away[0].shape[0] // 2
    qh, ql = (block_diagonal(q) for q in query)

    def against(part, high, low):
        left = [stack(a[part], k[part]) for a, k in zip(away, keys)]
        out = mm(side(*left), stack(high, high))
        return out + mm(left[0], low) if terms == 3 else out

    early = against(slice(0, half), qh, ql)
    later = against(slice(half, 2 * half), qh * late, ql * late)
    return early, later


def late_columns(tokens):
    lane = iota((PAIR, 2 * tokens), 1) % tokens
    return (lane >= tokens // 2).astype(F32).astype(BF16)


def cumulative(log_step):
    tokens = log_step.shape[0]
    shape = (tokens, tokens)
    lower = (iota(shape, 0) >= iota(shape, 1)).astype(F32).astype(BF16)
    high, low = split(log_step)
    lowest = (log_step - high.astype(F32) - low.astype(F32)).astype(BF16)
    return mm(side(lower, lower), stack(high, low)) + mm(lower, lowest)


def key_side(fade_ref, removal_ref, rate_ref, key_ref, ones, ready=lambda k: None):
    half = fade_ref.shape[0] // 2
    ready(0)
    log_step = -jnp.exp(fade_ref[...].astype(F32))
    cum = cumulative(log_step)
    middle = cum[half - 1 : half]
    inverse = jnp.exp(middle - cum)
    ready(1)
    removal = removal_ref[...].astype(F32)
    norm = group_sums(removal * removal, ones) * (1.0 / GROUP_DIMENSION)
    kappa = removal * lax.rsqrt(norm + KEY_EPS) * GROUP_DIMENSION ** (-0.5)
    ready(2)
    away = kappa * rate_ref[...].astype(F32) * inverse
    ready(3)
    keys = key_ref[...].astype(F32) * inverse
    return log_step, cum, middle, kappa, away, keys


def range_kernel(
    owners, fade_hbm, key_hbm, value_hbm, removal_hbm, rate_hbm, *rest
):
    send_refs = rest[:owners]
    solved_ref, loaded, held, load_sems, sems = rest[owners:]
    sources = (fade_hbm, removal_hbm, rate_hbm, key_hbm, value_hbm)
    loads = [
        pltpu.make_async_copy(source, loaded.at[k], load_sems.at[k])
        for k, source in enumerate(sources)
    ]
    for load in loads:
        load.start()
    fade_ref, removal_ref, rate_ref, key_ref, value_ref = (
        loaded.at[k] for k in range(len(sources))
    )
    me = lax.axis_index("seq")
    tokens, width = fade_ref.shape
    pairs = width // PAIR
    per_owner = held.shape[1]
    d = GROUP_DIMENSION

    ones = group_ones()
    late = late_columns(tokens)
    log_step, cum, middle, kappa, away, keys = key_side(
        fade_ref, removal_ref, rate_ref, key_ref, ones, lambda k: loads[k].wait()
    )
    loads[4].wait()
    end = cum[tokens - 1 : tokens]
    before = cum - log_step
    to_end = jnp.exp(end - middle)
    gamma_end = jnp.exp(end)
    toward_mid = -kappa * jnp.exp(before - middle)
    toward_abs = -kappa * jnp.exp(before)
    value = value_ref[...].astype(F32)

    cuts = [slice(p * PAIR, (p + 1) * PAIR) for p in range(pairs)]
    block = iota((d, 2 * PAIR), 1) % PAIR
    is_low = block < d
    strict = iota((d, 2 * PAIR), 0) < block % d
    low = (iota((d, PAIR), 1) < d).astype(F32).astype(BF16)
    high = (iota((d, PAIR), 1) >= d).astype(F32).astype(BF16)

    known, values, within, across, powers = [], [], [], [], []
    for cut in cuts:
        early, later = scores(
            late,
            split(away[:, cut]),
            split(keys[:, cut]),
            split(toward_mid[:, cut].T),
            2,
        )
        mix_early, mix_later = early[:d], later[:d]
        power = jnp.where(strict, jnp.where(is_low, mix_early, mix_later), 0.0)
        within.append(power)
        powers.append(power.astype(BF16))
        across.append(jnp.where(is_low, 0.0, mix_early))
        key_early, key_later = early[d:], later[d:]
        key_early = jnp.where(is_low & ~strict, 0.0, key_early)
        key_later = jnp.where(~is_low & strict, key_later, 0.0)
        mixed = stack(key_early.astype(BF16), key_later.astype(BF16))
        none = jnp.zeros((tokens, tokens), BF16)
        mixed = stack(side(mixed[:, :tokens], none), side(none, mixed[:, tokens:]))
        start = toward_abs[:, cut].T
        value_t = value[:, cut].T.astype(BF16)
        moved = mm(side(value_t[:d], value_t[d:]), mixed)
        known.append(stack(side(start[:d], start[d:]), moved))
        values.append(value_t)

    reach = 1
    while reach < d:
        for p in range(pairs):
            factor = lane_blocks(powers[p], low, high)
            if reach == 1:
                powers[p] = mm(powers[p], factor).astype(BF16)
            elif reach * 2 < d:
                out = mm(stack(within[p].astype(BF16), powers[p]), factor)
                within[p] = within[p] + powers[p].astype(F32) + out[:d]
                powers[p] = out[d:].astype(BF16)
            else:
                out = mm(within[p].astype(BF16), factor)
                within[p] = within[p] + powers[p].astype(F32) + out
        reach *= 2
    solved = []
    for p in range(pairs):
        factor = lane_blocks(within[p].astype(BF16), low, high)
        left = stack(known[p].astype(BF16), across[p].astype(BF16))
        out = mm(left, factor)
        solved.append(known[p] + out[:tokens])
        across[p] = (across[p] + out[tokens:]).astype(BF16)
    for p in range(pairs):
        one, two = across[p][:, :PAIR], across[p][:, PAIR:]
        none = jnp.zeros_like(one)
        factor = stack(side(one, none), side(none, none), side(none, two), side(none, none))
        solved[p] = (solved[p] + mm(solved[p].astype(BF16), factor)).astype(BF16)

    lane = iota((d, PAIR), 1)
    sub = iota((d, PAIR), 0)
    none = jnp.zeros((d, PAIR), BF16)
    for p, cut in enumerate(cuts):
        away_end = side(*split(away[:, cut] * to_end[:, cut]))
        keys_end = side(*split(keys[:, cut] * to_end[:, cut]))
        lefts = [
            side(
                solved[p][:, i * tokens : (i + 1) * tokens],
                stack(none, values[p][i * d : (i + 1) * d]),
            )
            for i in range(2)
        ]
        ended = folded(stack(*lefts), stack(away_end, keys_end))
        for i in range(2):
            solved_ref[2 * p + i] = lefts[i]
            stay = jnp.where(lane == sub + i * d, gamma_end[:, cut], 0.0)
            state_map = ended[2 * i * d : (2 * i + 1) * d] + stay
            state_add = ended[(2 * i + 1) * d : (2 * i + 2) * d]
            if i == 0:
                state_add = pltpu.roll(state_add, d, 1)
            else:
                state_map = pltpu.roll(state_map, d, 1)
            head = 2 * p + i
            slot = lax.rem(head // per_owner - me % owners + owners, owners)
            held[slot, head % per_owner] = jnp.where(
                lane < d, state_map, state_add
            )

    copies = [
        pltpu.make_async_copy(held.at[k], send_refs[k], sems.at[k])
        for k in range(owners)
    ]
    for copy in copies:
        copy.start()
    for copy in copies:
        copy.wait()


def resident(count):
    return [pl.BlockSpec(memory_space=pltpu.VMEM)] * count


def limit(mib):
    return pltpu.CompilerParams(vmem_limit_bytes=mib << 20)


def range_pass(owners, fade, key, value, removal, rate):
    tokens, features = fade.shape
    heads = features // GROUP_DIMENSION
    block = (heads // owners, GROUP_DIMENSION, PAIR)
    out = pl.pallas_call(
        functools.partial(range_kernel, owners),
        in_specs=[pl.BlockSpec(memory_space=pltpu.HBM)] * 5,
        out_specs=[pl.BlockSpec(memory_space=pl.ANY)] * owners + resident(2),
        out_shape=[jax.ShapeDtypeStruct(block, F32)] * owners
        + [
            jax.ShapeDtypeStruct((heads, tokens, 2 * tokens), BF16),
            jax.ShapeDtypeStruct((5, tokens, features), BF16),
        ],
        scratch_shapes=[
            pltpu.VMEM((owners,) + block, F32),
            pltpu.SemaphoreType.DMA((5,)),
            pltpu.SemaphoreType.DMA((owners,)),
        ],
        compiler_params=limit(40),
        name="range_pass",
    )(fade, key, value, removal, rate)
    return out[:owners], out[owners:]


def read_kernel(
    reader_ref,
    extra_ref,
    solved_ref,
    loaded,
    lift_high_ref,
    lift_low_ref,
    within_ref,
    bonus_ref,
):
    fade_ref, removal_ref, rate_ref, key_ref, value_ref = (
        loaded.at[k] for k in range(loaded.shape[0])
    )
    tokens, width = fade_ref.shape
    d = GROUP_DIMENSION
    ones = group_ones()
    late = late_columns(tokens)
    seen = iota((tokens, tokens), 0) <= iota((tokens, tokens), 1)
    _, cum, middle, _, away, keys = key_side(
        fade_ref, removal_ref, rate_ref, key_ref, ones
    )
    reader = reader_ref[...].astype(F32)
    value = value_ref[...].astype(F32)
    bonus = group_sums(reader * key_ref[...].astype(F32) * extra_ref[...], ones)
    bonus_ref[...] = bonus * value
    reader_mid = reader * jnp.exp(cum - middle)
    reader_abs = reader * jnp.exp(cum)

    for p in range(width // PAIR):
        cut = slice(p * PAIR, (p + 1) * PAIR)
        early, later = scores(
            late,
            split(away[:, cut]),
            split(keys[:, cut]),
            split(reader_mid[:, cut].T),
            3,
        )
        start = reader_abs[:, cut].T
        for i in range(2):
            lanes = slice(i * tokens, (i + 1) * tokens)
            rows = slice(i * d, (i + 1) * d)
            at = slice(p * PAIR + i * d, p * PAIR + (i + 1) * d)

            def read(part):
                whole = stack(early[part, lanes], later[part, lanes])
                return side(*split(jnp.where(seen, whole, 0.0)))

            out = folded(
                solved_ref[2 * p + i], stack(read(slice(0, d)), read(slice(d, 2 * d)))
            )
            within_ref[at] = out[d:]
            lift_high_ref[at], lift_low_ref[at] = split(start[rows] + out[:d])


def read_pass(reader, extra, solved, loaded):
    tokens, features = reader.shape
    return pl.pallas_call(
        read_kernel,
        in_specs=resident(4),
        out_specs=resident(4),
        out_shape=[
            jax.ShapeDtypeStruct((features, tokens), BF16),
            jax.ShapeDtypeStruct((features, tokens), BF16),
            jax.ShapeDtypeStruct((features, tokens), F32),
            jax.ShapeDtypeStruct((tokens, features), F32),
        ],
        compiler_params=limit(40),
        name="read_pass",
    )(reader, extra, solved, loaded)


def chain_kernel(owners, *refs):
    got_refs = refs[:owners]
    state_refs = refs[owners : 2 * owners]
    final_ref, ranges, states = refs[2 * owners :]
    me = lax.axis_index("seq")
    per_owner = got_refs[0].shape[0]
    for k in range(owners):
        ranges[lax.rem(me - k + owners, owners)] = got_refs[k][...]
    d = GROUP_DIMENSION
    lane = iota((d // 2, PAIR), 1)
    none = jnp.zeros((d, 2 * PAIR), BF16)
    current = []
    for q in range(per_owner):
        states[0, q] = jnp.zeros((d // 2, PAIR), F32)
        current.append(ranges[0, q])
    for i in range(1, owners):
        for q in range(per_owner):
            now = current[q]
            states[i, q] = jnp.where(
                lane < d, pltpu.roll(now[: d // 2], d, 1), now[d // 2 :]
            )
            both = ranges[i, q]
            maps = side(*split(pltpu.roll(both, d, 1)))
            out = mm(stack(*split(now)), stack(none, maps))
            current[q] = out[:d, :PAIR] + out[:d, PAIR:] + out[d:, :PAIR] + both
    for q in range(per_owner):
        final_ref[q * d : (q + 1) * d, :] = pltpu.roll(current[q], d, 1)[:, :d]
    for k in range(owners):
        state_refs[k][...] = states[lax.rem(me + k, owners)]


def chain(got):
    owners = len(got)
    per_owner = got[0].shape[0]
    block = (per_owner, GROUP_DIMENSION // 2, PAIR)
    rows = per_owner * GROUP_DIMENSION
    out = pl.pallas_call(
        functools.partial(chain_kernel, owners),
        in_specs=resident(owners),
        out_specs=resident(owners + 1),
        out_shape=[jax.ShapeDtypeStruct(block, F32)] * owners
        + [jax.ShapeDtypeStruct((rows, GROUP_DIMENSION), F32)],
        scratch_shapes=[
            pltpu.VMEM((owners,) + got[0].shape, F32),
            pltpu.VMEM((owners,) + block, F32),
        ],
        compiler_params=limit(40),
        name="chain",
    )(*got)
    return out[:owners], out[owners]


def finish_kernel(owners, *refs):
    state_refs = refs[:owners]
    lift_high_ref, lift_low_ref, within_ref, bonus_ref, gain_ref = refs[
        owners : owners + 5
    ]
    out_ref, states = refs[owners + 5 :]
    me = lax.axis_index("seq")
    per_owner = state_refs[0].shape[0]
    width = out_ref.shape[1]
    d = GROUP_DIMENSION

    for k in range(owners):
        states[lax.rem(me % owners - k + owners, owners)] = state_refs[k][...]

    lane = iota((d // 2, PAIR), 1)
    for p in range(width // PAIR):
        normed = []
        for i in range(2):
            head = 2 * p + i
            packed = states[head // per_owner, head % per_owner]
            state = split(
                stack(
                    jnp.where(lane < d, packed, 0.0),
                    jnp.where(lane >= d, packed, 0.0),
                )
            )
            at = slice(p * PAIR + i * d, p * PAIR + (i + 1) * d)
            high, low = lift_high_ref[at], lift_low_ref[at]
            result = within_ref[at] + mm3(
                state, (stack(high, high), stack(low, low))
            )
            average = jnp.mean(result, axis=0, keepdims=True)
            centered = result - average
            spread = jnp.mean(centered * centered, axis=0, keepdims=True)
            normed.append(centered * lax.rsqrt(spread + NORM_EPS))
        cut = slice(p * PAIR, (p + 1) * PAIR)
        turned = stack(*normed).T
        out_ref[:, cut] = (turned * gain_ref[:, cut] + bonus_ref[:, cut]).astype(BF16)


def finish(states, lift_high, lift_low, within, bonus, gain):
    owners = len(states)
    tokens, features = bonus.shape
    return pl.pallas_call(
        functools.partial(finish_kernel, owners),
        in_specs=resident(owners + 5),
        out_specs=resident(1)[0],
        out_shape=jax.ShapeDtypeStruct((tokens, features), BF16),
        scratch_shapes=[pltpu.VMEM((owners,) + states[0].shape, F32)],
        compiler_params=limit(40),
        name="finish",
    )(*states, lift_high, lift_low, within, bonus, gain)


def shifted(value, by, members):
    return lax.ppermute(value, "seq", [(i, (i + by) % members) for i in range(members)])


def relay_states(both, members):
    d = GROUP_DIMENSION
    local_map, local_add = both[:, :, :d], both[:, :, d:]

    def relay(_, carried):
        pairs = [(i, i + 1) for i in range(members - 1)]
        incoming = lax.ppermute(carried[1], "seq", pairs)
        moved = jnp.einsum(
            "hvk,hkj->hvj", incoming, local_map, precision=lax.Precision.HIGHEST
        )
        return (incoming, moved + local_add)

    first = (jnp.zeros_like(local_add), local_add)
    incoming, leaving = lax.fori_loop(0, members - 1, relay, first)
    here = lax.axis_index("seq")
    closing = lax.psum(jnp.where(here == members - 1, leaving, 0.0), "seq")
    closing = closing.reshape(-1, d)
    rows = closing.shape[0] // members
    final = lax.dynamic_slice_in_dim(closing, here * rows, rows, 0)
    packed = jnp.concatenate([incoming[:, : d // 2], incoming[:, d // 2 :]], axis=2)
    return packed, final


def on_device(reader, fade, key, value, removal, rate, extra, gain):
    members = lax.axis_size("seq")
    features = reader.shape[2]
    heads = features // GROUP_DIMENSION
    owners = members if heads % members == 0 else 1
    keyed = (fade[0], key[0], value[0], removal[0], rate[0])
    keyed = [pltpu.with_memory_space_constraint(x, pltpu.HBM) for x in keyed]
    sends, kept = range_pass(owners, *keyed)
    parts = read_pass(reader[0], extra.reshape(1, features), *kept)
    if owners > 1:
        got = [sends[0]] + [shifted(sends[k], k, members) for k in range(1, owners)]
        got, parts = lax.optimization_barrier((got, parts))
        states, final = chain(got)
        states = [states[0]] + [
            shifted(states[k], k, members) for k in range(1, owners)
        ]
    else:
        packed, final = relay_states(sends[0], members)
        states = [packed]
    blended = finish(states, *parts, gain.reshape(1, features))
    return (blended[None], final[None])


def solution(mesh):
    tokens = P(("groups", "dp"), "seq", None)
    return jax.shard_map(
        on_device,
        mesh=mesh,
        in_specs=(tokens,) * 6 + (P(), P()),
        out_specs=(tokens, tokens),
        check_vma=False,
    )
```

time: 47 us -> 38.4 us (0.82)
  Pallas kernels: 23.1 us -> 13.4 us
  waiting for transfers between devices: 5.45 us -> 9.89 us
  local copies, waits for them, and re-layouts: 4.26 us -> 0.78 us
    pallas_call x4, Pallas kernels: 23.1 us -> 13.4 us  [the longest x1 7.4 us: range_pass(): pl.pallas_call(functools.partial(range_kernel, owners), in_specs=[pl.Bloc...]
    ppermute x6, waiting for transfers between devices: 5.45 us -> 9.89 us  [shifted(): lax.ppermute(value, 'seq', [(i, (i + by) % members) for i in range(member...]
    unnamed x17 -> x7, local copies, waits for them, and re-layouts: 3.07 us -> 0.77 us
    reshape x1, local copies, waits for them, and re-layouts: 0.6 us -> 0.01 us  [on_device(): parts = read_pass(reader[0], extra.reshape(1, features), *kept)]
    reshape x1, local copies, waits for them, and re-layouts: 0.59 us -> 0.01 us  [on_device(): blended = finish(states, *parts, gain.reshape(1, features))]
  transfers between devices with their start and end apart: 6 -> 6, of which waited for: 3 -> 4; matrix products, arithmetic and copies ran while one was open for 6% -> 2% of each run, Pallas kernels for 14% -> 10%
where the time goes in v3:
time: 38.4 us; the launch traced here: 38.3 us
  starting transfers between devices  13.5 us (35%)
  Pallas kernels  13.4 us (35%)
  waiting for transfers between devices  9.89 us (26%)
  local copies, waits for them, and re-layouts  0.78 us (2%)
  between operations  0.7 us (2%)
    ppermute x6, starting transfers between devices, shifted(): lax.ppermute(value, 'seq', [(i, (i + by) % members) for i in range(member...  13.5 us
    ppermute x6, waiting for transfers between devices, shifted(): lax.ppermute(value, 'seq', [(i, (i + by) % members) for i in range(member...  9.89 us
    pallas_call x1, Pallas kernels, range_pass(): pl.pallas_call(functools.partial(range_kernel, owners), in_specs=[pl.Bloc...  7.4 us
    pallas_call x1, Pallas kernels, read_pass(): pl.pallas_call(read_kernel, in_specs=resident(4), out_specs=resident(4),...  3.87 us
    pallas_call x1, Pallas kernels, finish(): pl.pallas_call(functools.partial(finish_kernel, owners), in_specs=residen...  1.37 us
    unnamed x7, local copies, waits for them, and re-layouts  0.77 us
  transfers between devices with their start and end apart: 6, of which 4 were waited for; matrix products, arithmetic and copies ran while one was open for 2% of the time, Pallas kernels for 10%

profile of v3, /device:TPU:0, one launch (start us, length us, event | category | flops | bytes accessed | tf_op | source)
XLA Modules:
  0.0 38.3 jit_solution(18052288242389183881)
XLA Ops:
  0.6 0.0 copy-start.1
  0.6 0.0 copy-start
  0.7 7.4 %range_pass.1 = (f32[5,64,128]{2,1,0:T(8,128)S(1)}, f32[5,64,128]{2,1,0:T(8,128)S(1)}, f32[5,64,128]{2,1,0:T(8,128)S(1)}, f32[5,64,128]{2,1,0:T(8,128)S(1)}, bf1...) custom-call(bf16[128,1280]{1,0:T(8,128)(2,1)} %bitcast.11, bf16[128,1280]{1,0:T(8,128)(2,1)} %bitcast.12, ...), custom_call_target="tpu_custom_call" | custom-call | tf_op jit(solution)/shard_map/range_pass/pallas_call | solution.py:276
  8.1 3.1 %collective-permute-start = (f32[5,64,128]{2,1,0:T(8,128)S(1)}, f32[5,64,128]{2,1,0:T(8,128)S(1)}, u32[]{:S(2)}, u32[]{:S(2)}) collective-permute-start(f32[5,64,128]{2,1,0:T(8,128)S(1)} %get-tuple-element.26), channel_id=1, source_target_pairs={{0,4},{4,8},{8,12},{12,0},{1,5},{5,9},{9,13},{13,1},{2,6},{6,10},{... | collective-permute-start | bytes 491528 | tf_op jit(solution)/shard_map/ppermute | solution.py:474
  11.2 2.6 %collective-permute-start.1 = (f32[5,64,128]{2,1,0:T(8,128)S(1)}, f32[5,64,128]{2,1,0:T(8,128)S(1)}, u32[]{:S(2)}, u32[]{:S(2)}) collective-permute-start(f32[5,64,128]{2,1,0:T(8,128)S(1)} %get-tuple-element.27), channel_id=1, source_target_pairs={{0,8},{4,12},{8,0},{12,4},{1,9},{5,13},{9,1},{13,5},{2,10},{6,14},... | collective-permute-start | bytes 491528 | tf_op jit(solution)/shard_map/ppermute | solution.py:474
  13.8 1.3 %collective-permute-start.2 = (f32[5,64,128]{2,1,0:T(8,128)S(1)}, f32[5,64,128]{2,1,0:T(8,128)S(1)}, u32[]{:S(2)}, u32[]{:S(2)}) collective-permute-start(f32[5,64,128]{2,1,0:T(8,128)S(1)} %get-tuple-element.28), channel_id=1, source_target_pairs={{0,12},{4,0},{8,4},{12,8},{1,13},{5,1},{9,5},{13,9},{2,14},{6,2},{... | collective-permute-start | bytes 491528 | tf_op jit(solution)/shard_map/ppermute | solution.py:474
  15.1 0.0 copy-done.1
  15.1 0.0 copy-done
  15.1 0.0 copy-start.2
  15.1 3.9 %read_pass.1 = (bf16[1280,128]{1,0:T(8,128)(2,1)S(1)}, bf16[1280,128]{1,0:T(8,128)(2,1)S(1)}, f32[1280,128]{1,0:T(8,128)S(1)}, f32[128,1280]{1,0:T(8,128)S(1)}) custom-call(bf16[128,1280]{1,0:T(8,128)(2,1)S(1)} %bitcast.8, f32[1,1280]{1,0:T(1,128)S(1)} %reshape.10.extra_ref, bf16[20,128,256]{2,1,0:T(8,128)(2,1)S(1)} %get-tuple-element.29.solved_ref, ...), custom_call_target="tpu_custom_call" | custom-call | tf_op jit(solution)/shard_map/read_pass/pallas_call | solution.py:352
  19.0 0.0 collective-permute-done.refs_1_
  19.0 5.5 %collective-permute-done.1.refs_2_ = f32[5,64,128]{2,1,0:T(8,128)S(1)} collective-permute-done((f32[5,64,128]{2,1,0:T(8,128)S(1)}, f32[5,64,128]{2,1,0:T(8,128)S(1)}, u32[]{:S(2)}, u32[]{:S(2)}) %collective-permute-start.1) | collective-permute-done | bytes 163872 | tf_op jit(solution)/shard_map/ppermute | solution.py:474
  24.5 0.0 collective-permute-done.2.refs_3_
  24.5 0.7 %chain.1 = (f32[5,32,128]{2,1,0:T(8,128)S(1)}, f32[5,32,128]{2,1,0:T(8,128)S(1)}, f32[5,32,128]{2,1,0:T(8,128)S(1)}, f32[5,32,128]{2,1,0:T(8,128)S(1)}, f32[320,64]{1,0:T(8,128)S(1)}) custom-call(f32[5,64,128]{2,1,0:T(8,128)S(1)} %get-tuple-element.35.refs_0_, f32[5,64,128]{2,1,0:T(8,128)S(1)} %collective-permute-done.refs_1_, ...), custom_call_target="tpu_custom_call" | custom-call | tf_op jit(solution)/shard_map/chain/pallas_call | solution.py:403
  25.2 4.0 %collective-permute-start.3 = (f32[5,32,128]{2,1,0:T(8,128)S(1)}, f32[5,32,128]{2,1,0:T(8,128)S(1)}, u32[]{:S(2)}, u32[]{:S(2)}) collective-permute-start(f32[5,32,128]{2,1,0:T(8,128)S(1)} %get-tuple-element.40), channel_id=1, source_target_pairs={{0,4},{4,8},{8,12},{12,0},{1,5},{5,9},{9,13},{13,1},{2,6},{6,10},{... | collective-permute-start | bytes 245768 | tf_op jit(solution)/shard_map/ppermute | solution.py:474
  29.3 1.6 %collective-permute-start.4 = (f32[5,32,128]{2,1,0:T(8,128)S(1)}, f32[5,32,128]{2,1,0:T(8,128)S(1)}, u32[]{:S(2)}, u32[]{:S(2)}) collective-permute-start(f32[5,32,128]{2,1,0:T(8,128)S(1)} %get-tuple-element.41), channel_id=1, source_target_pairs={{0,8},{4,12},{8,0},{12,4},{1,9},{5,13},{9,1},{13,5},{2,10},{6,14},... | collective-permute-start | bytes 245768 | tf_op jit(solution)/shard_map/ppermute | solution.py:474
  30.9 0.8 %collective-permute-start.5 = (f32[5,32,128]{2,1,0:T(8,128)S(1)}, f32[5,32,128]{2,1,0:T(8,128)S(1)}, u32[]{:S(2)}, u32[]{:S(2)}) collective-permute-start(f32[5,32,128]{2,1,0:T(8,128)S(1)} %get-tuple-element.42), channel_id=1, source_target_pairs={{0,12},{4,0},{8,4},{12,8},{1,13},{5,1},{9,5},{13,9},{2,14},{6,2},{... | collective-permute-start | bytes 245768 | tf_op jit(solution)/shard_map/ppermute | solution.py:474
  31.7 0.0 copy-done.2
  31.7 0.8 %copy.10 = f32[1,320,64]{1,2,0:T(8,128)} copy(f32[1,320,64]{2,1,0:T(8,128)S(1)} %bitcast.9) | data formatting | bytes 163840
  32.5 0.8 %collective-permute-done.3.refs_1_ = f32[5,32,128]{2,1,0:T(8,128)S(1)} collective-permute-done((f32[5,32,128]{2,1,0:T(8,128)S(1)}, f32[5,32,128]{2,1,0:T(8,128)S(1)}, u32[]{:S(2)}, u32[]{:S(2)}) %collective-permute-start.3) | collective-permute-done | bytes 81952 | tf_op jit(solution)/shard_map/ppermute | solution.py:474
  33.3 3.1 %collective-permute-done.4.refs_2_ = f32[5,32,128]{2,1,0:T(8,128)S(1)} collective-permute-done((f32[5,32,128]{2,1,0:T(8,128)S(1)}, f32[5,32,128]{2,1,0:T(8,128)S(1)}, u32[]{:S(2)}, u32[]{:S(2)}) %collective-permute-start.4) | collective-permute-done | bytes 81952 | tf_op jit(solution)/shard_map/ppermute | solution.py:474
  36.4 0.5 %collective-permute-done.5.refs_3_ = f32[5,32,128]{2,1,0:T(8,128)S(1)} collective-permute-done((f32[5,32,128]{2,1,0:T(8,128)S(1)}, f32[5,32,128]{2,1,0:T(8,128)S(1)}, u32[]{:S(2)}, u32[]{:S(2)}) %collective-permute-start.5) | collective-permute-done | bytes 81952 | tf_op jit(solution)/shard_map/ppermute | solution.py:474
  36.9 1.4 %finish.1 = bf16[128,1280]{1,0:T(8,128)(2,1)} custom-call(f32[5,32,128]{2,1,0:T(8,128)S(1)} %get-tuple-element.39.refs_0_, f32[5,32,128]{2,1,0:T(8,128)S(1)} %collective-permute-done.3.refs_1_, f32[5,32,128]{2,1,0:T(8,128)S(1)} %collective-permute-done.4.refs_2_, f32[5,32,128]{2,1,0:T(8,128)S(1)} %collective-permute-done.5.refs_3_, ...), custom_call_target="tpu_custom_call" | custom-call | tf_op jit(solution)/shard_map/finish/pallas_call | solution.py:462
  (2 shorter events, 0.0 us)
Async XLA Ops:
  0.6 14.5 %copy-start.1 = (f32[1280]{0:T(1024)S(1)}, f32[1280]{0:T(1024)}, u32[]{:S(2)}) copy-start(f32[1280]{0:T(1024)} %param.14) | copy-start | bytes 15364
  0.6 14.5 %copy-start = (bf16[1,128,1280]{2,1,0:T(8,128)(2,1)S(1)}, bf16[1,128,1280]{2,1,0:T(8,128)(2,1)}, u32[]{:S(2)}) copy-start(bf16[1,128,1280]{2,1,0:T(8,128)(2,1)} %param.8) | copy-start | bytes 983044
  8.1 11.0 %collective-permute-start = (f32[5,64,128]{2,1,0:T(8,128)S(1)}, f32[5,64,128]{2,1,0:T(8,128)S(1)}, u32[]{:S(2)}, u32[]{:S(2)}) collective-permute-start(f32[5,64,128]{2,1,0:T(8,128)S(1)} %get-tuple-element.26), channel_id=1, source_target_pairs={{0,4},{4,8},{8,12},{12,0},{1,5},{5,9},{9,13},{13,1},{2,6},{6,10},{... | collective-permute-start | bytes 491528 | tf_op jit(solution)/shard_map/ppermute | solution.py:474
  11.2 13.3 %collective-permute-start.1 = (f32[5,64,128]{2,1,0:T(8,128)S(1)}, f32[5,64,128]{2,1,0:T(8,128)S(1)}, u32[]{:S(2)}, u32[]{:S(2)}) collective-permute-start(f32[5,64,128]{2,1,0:T(8,128)S(1)} %get-tuple-element.27), channel_id=1, source_target_pairs={{0,8},{4,12},{8,0},{12,4},{1,9},{5,13},{9,1},{13,5},{2,10},{6,14},... | collective-permute-start | bytes 491528 | tf_op jit(solution)/shard_map/ppermute | solution.py:474
  13.8 10.8 %collective-permute-start.2 = (f32[5,64,128]{2,1,0:T(8,128)S(1)}, f32[5,64,128]{2,1,0:T(8,128)S(1)}, u32[]{:S(2)}, u32[]{:S(2)}) collective-permute-start(f32[5,64,128]{2,1,0:T(8,128)S(1)} %get-tuple-element.28), channel_id=1, source_target_pairs={{0,12},{4,0},{8,4},{12,8},{1,13},{5,1},{9,5},{13,9},{2,14},{6,2},{... | collective-permute-start | bytes 491528 | tf_op jit(solution)/shard_map/ppermute | solution.py:474
  15.1 16.6 %copy-start.2 = (f32[1280]{0:T(1024)S(1)}, f32[1280]{0:T(1024)}, u32[]{:S(2)}) copy-start(f32[1280]{0:T(1024)} %param.15) | copy-start | bytes 15364
  25.2 8.1 %collective-permute-start.3 = (f32[5,32,128]{2,1,0:T(8,128)S(1)}, f32[5,32,128]{2,1,0:T(8,128)S(1)}, u32[]{:S(2)}, u32[]{:S(2)}) collective-permute-start(f32[5,32,128]{2,1,0:T(8,128)S(1)} %get-tuple-element.40), channel_id=1, source_target_pairs={{0,4},{4,8},{8,12},{12,0},{1,5},{5,9},{9,13},{13,1},{2,6},{6,10},{... | collective-permute-start | bytes 245768 | tf_op jit(solution)/shard_map/ppermute | solution.py:474
  29.3 7.1 %collective-permute-start.4 = (f32[5,32,128]{2,1,0:T(8,128)S(1)}, f32[5,32,128]{2,1,0:T(8,128)S(1)}, u32[]{:S(2)}, u32[]{:S(2)}) collective-permute-start(f32[5,32,128]{2,1,0:T(8,128)S(1)} %get-tuple-element.41), channel_id=1, source_target_pairs={{0,8},{4,12},{8,0},{12,4},{1,9},{5,13},{9,1},{13,5},{2,10},{6,14},... | collective-permute-start | bytes 245768 | tf_op jit(solution)/shard_map/ppermute | solution.py:474
  30.9 6.0 %collective-permute-start.5 = (f32[5,32,128]{2,1,0:T(8,128)S(1)}, f32[5,32,128]{2,1,0:T(8,128)S(1)}, u32[]{:S(2)}, u32[]{:S(2)}) collective-permute-start(f32[5,32,128]{2,1,0:T(8,128)S(1)} %get-tuple-element.42), channel_id=1, source_target_pairs={{0,12},{4,0},{8,4},{12,8},{1,13},{5,1},{9,5},{13,9},{2,14},{6,2},{... | collective-permute-start | bytes 245768 | tf_op jit(solution)/shard_map/ppermute | solution.py:474

commit v4 on v3

--- a/solution.py
+++ b/solution.py
@@ -18,6 +18,12 @@
 
 def mm(left, right):
     return jnp.dot(left, right, preferred_element_type=F32)
+
+
+def mm_turned(left, right):
+    return lax.dot_general(
+        left, right, (((1,), (1,)), ((), ())), preferred_element_type=F32
+    )
 
 
 def split(x):
@@ -104,9 +110,7 @@
     tokens = log_step.shape[0]
     shape = (tokens, tokens)
     lower = (iota(shape, 0) >= iota(shape, 1)).astype(F32).astype(BF16)
-    high, low = split(log_step)
-    lowest = (log_step - high.astype(F32) - low.astype(F32)).astype(BF16)
-    return mm(side(lower, lower), stack(high, low)) + mm(lower, lowest)
+    return mm(side(lower, lower), stack(*split(log_step)))
 
 
 def key_side(fade_ref, removal_ref, rate_ref, key_ref, ones, ready=lambda k: None):
@@ -115,16 +119,15 @@
     log_step = -jnp.exp(fade_ref[...].astype(F32))
     cum = cumulative(log_step)
     middle = cum[half - 1 : half]
-    inverse = jnp.exp(middle - cum)
+    past = cum - middle
+    inverse = jnp.exp(-past)
     ready(1)
     removal = removal_ref[...].astype(F32)
     norm = group_sums(removal * removal, ones) * (1.0 / GROUP_DIMENSION)
     kappa = removal * lax.rsqrt(norm + KEY_EPS) * GROUP_DIMENSION ** (-0.5)
-    ready(2)
     away = kappa * rate_ref[...].astype(F32) * inverse
-    ready(3)
     keys = key_ref[...].astype(F32) * inverse
-    return log_step, cum, middle, kappa, away, keys
+    return log_step, cum, middle, past, kappa, away, keys
 
 
 def range_kernel(
@@ -139,6 +142,11 @@
     ]
     for load in loads:
         load.start()
+
+    def ready(stage):
+        for load in loads[:1] if stage == 0 else loads[1:]:
+            load.wait()
+
     fade_ref, removal_ref, rate_ref, key_ref, value_ref = (
         loaded.at[k] for k in range(len(sources))
     )
@@ -149,48 +157,60 @@
     d = GROUP_DIMENSION
 
     ones = group_ones()
-    late = late_columns(tokens)
-    log_step, cum, middle, kappa, away, keys = key_side(
-        fade_ref, removal_ref, rate_ref, key_ref, ones, lambda k: loads[k].wait()
-    )
-    loads[4].wait()
+    log_step, cum, middle, past, kappa, away, keys = key_side(
+        fade_ref, removal_ref, rate_ref, key_ref, ones, ready
+    )
     end = cum[tokens - 1 : tokens]
-    before = cum - log_step
     to_end = jnp.exp(end - middle)
     gamma_end = jnp.exp(end)
-    toward_mid = -kappa * jnp.exp(before - middle)
-    toward_abs = -kappa * jnp.exp(before)
-    value = value_ref[...].astype(F32)
+    toward_mid = -kappa * jnp.exp(past - log_step)
+    toward_abs = toward_mid * jnp.exp(middle)
 
     cuts = [slice(p * PAIR, (p + 1) * PAIR) for p in range(pairs)]
     block = iota((d, 2 * PAIR), 1) % PAIR
     is_low = block < d
     strict = iota((d, 2 * PAIR), 0) < block % d
+    unit = iota((d, 2 * PAIR), 0) == block % d
     low = (iota((d, PAIR), 1) < d).astype(F32).astype(BF16)
     high = (iota((d, PAIR), 1) >= d).astype(F32).astype(BF16)
 
-    known, values, within, across, powers = [], [], [], [], []
+    lanes = iota((tokens, PAIR), 1)
+    low_rows = (lanes < d).astype(F32).astype(BF16)
+    high_rows = (lanes >= d).astype(F32).astype(BF16)
+    late_rows = (iota((tokens, PAIR), 0) >= tokens // 2).astype(F32).astype(BF16)
+    eye = (iota((PAIR, PAIR), 0) == iota((PAIR, PAIR), 1)).astype(F32).astype(BF16)
+    known, values, inverses, across, powers = [], [], [], [], []
+    scored = []
     for cut in cuts:
-        early, later = scores(
-            late,
-            split(away[:, cut]),
-            split(keys[:, cut]),
-            split(toward_mid[:, cut].T),
-            2,
-        )
+        query = toward_mid[:, cut].astype(BF16)
+        own = low_rows, high_rows
+        every = stack(*(query * mask for mask in own))
+        recent = stack(*(query * late_rows * mask for mask in own))
+        a_parts, k_parts = split(away[:, cut]), split(keys[:, cut])
+
+        def against(part, queries):
+            lefts = [stack(a[part], k[part]) for a, k in zip(a_parts, k_parts)]
+            return mm_turned(side(*lefts), side(queries, queries))
+
+        scored.append((against(slice(0, d), every), against(slice(d, 2 * d), recent)))
+    turned = [
+        mm_turned(eye, stack(toward_abs[:, cut].astype(BF16), value_ref[:, cut]))
+        for cut in cuts
+    ]
+    mixes = []
+    for early, later in scored:
         mix_early, mix_later = early[:d], later[:d]
         power = jnp.where(strict, jnp.where(is_low, mix_early, mix_later), 0.0)
-        within.append(power)
+        inverses.append(jnp.where(unit, 1.0, power))
         powers.append(power.astype(BF16))
         across.append(jnp.where(is_low, 0.0, mix_early))
-        key_early, key_later = early[d:], later[d:]
-        key_early = jnp.where(is_low & ~strict, 0.0, key_early)
-        key_later = jnp.where(~is_low & strict, key_later, 0.0)
-        mixed = stack(key_early.astype(BF16), key_later.astype(BF16))
-        none = jnp.zeros((tokens, tokens), BF16)
+        key_early = jnp.where(is_low & ~strict, 0.0, early[d:])
+        key_later = jnp.where(~is_low & strict, later[d:], 0.0)
+        mixes.append(stack(key_early.astype(BF16), key_later.astype(BF16)))
+    none = jnp.zeros((tokens, tokens), BF16)
+    for both, mixed in zip(turned, mixes):
+        start, value_t = both[:, :tokens], both[:, tokens:].astype(BF16)
         mixed = stack(side(mixed[:, :tokens], none), side(none, mixed[:, tokens:]))
-        start = toward_abs[:, cut].T
-        value_t = value[:, cut].T.astype(BF16)
         moved = mm(side(value_t[:d], value_t[d:]), mixed)
         known.append(stack(side(start[:d], start[d:]), moved))
         values.append(value_t)
@@ -202,16 +222,16 @@
             if reach == 1:
                 powers[p] = mm(powers[p], factor).astype(BF16)
             elif reach * 2 < d:
-                out = mm(stack(within[p].astype(BF16), powers[p]), factor)
-                within[p] = within[p] + powers[p].astype(F32) + out[:d]
+                out = mm(stack(inverses[p].astype(BF16), powers[p]), factor)
+                inverses[p] = inverses[p] + out[:d]
                 powers[p] = out[d:].astype(BF16)
             else:
-                out = mm(within[p].astype(BF16), factor)
-                within[p] = within[p] + powers[p].astype(F32) + out
+                inverses[p] = inverses[p] + mm(inverses[p].astype(BF16), factor)
         reach *= 2
     solved = []
     for p in range(pairs):
-        factor = lane_blocks(within[p].astype(BF16), low, high)
+        rest = jnp.where(strict, inverses[p], 0.0).astype(BF16)
+        factor = lane_blocks(rest, low, high)
         left = stack(known[p].astype(BF16), across[p].astype(BF16))
         out = mm(left, factor)
         solved.append(known[p] + out[:tokens])
@@ -226,7 +246,8 @@
     sub = iota((d, PAIR), 0)
     none = jnp.zeros((d, PAIR), BF16)
     for p, cut in enumerate(cuts):
-        away_end = side(*split(away[:, cut] * to_end[:, cut]))
+        away_end = (away[:, cut] * to_end[:, cut]).astype(BF16)
+        away_end = side(away_end, jnp.zeros_like(away_end))
         keys_end = side(*split(keys[:, cut] * to_end[:, cut]))
         lefts = [
             side(
@@ -311,15 +332,15 @@
     ones = group_ones()
     late = late_columns(tokens)
     seen = iota((tokens, tokens), 0) <= iota((tokens, tokens), 1)
-    _, cum, middle, _, away, keys = key_side(
+    _, cum, middle, past, _, away, keys = key_side(
         fade_ref, removal_ref, rate_ref, key_ref, ones
     )
     reader = reader_ref[...].astype(F32)
     value = value_ref[...].astype(F32)
     bonus = group_sums(reader * key_ref[...].astype(F32) * extra_ref[...], ones)
     bonus_ref[...] = bonus * value
-    reader_mid = reader * jnp.exp(cum - middle)
-    reader_abs = reader * jnp.exp(cum)
+    reader_mid = reader * jnp.exp(past)
+    reader_abs = reader_mid * jnp.exp(middle)
 
     for p in range(width // PAIR):
         cut = slice(p * PAIR, (p + 1) * PAIR)

time: 38.4 us -> 37.1 us (0.966)
  Pallas kernels: 13.4 us -> 11.9 us
    pallas_call x1, Pallas kernels: 7.4 us -> 6.13 us  [range_pass(): pl.pallas_call(functools.partial(range_kernel, owners), in_specs=[pl.Bloc...]
where the time goes in v4:
time: 37.1 us; the launch traced here: 37 us
  starting transfers between devices  13.5 us (36%)
  Pallas kernels  11.9 us (32%)
  waiting for transfers between devices  10.1 us (27%)
  local copies, waits for them, and re-layouts  0.78 us (2%)
  between operations  0.7 us (2%)
    ppermute x6, starting transfers between devices, shifted(): lax.ppermute(value, 'seq', [(i, (i + by) % members) for i in range(member...  13.5 us
    ppermute x6, waiting for transfers between devices, shifted(): lax.ppermute(value, 'seq', [(i, (i + by) % members) for i in range(member...  10.1 us
    pallas_call x1, Pallas kernels, range_pass(): pl.pallas_call(functools.partial(range_kernel, owners), in_specs=[pl.Bloc...  6.13 us
    pallas_call x1, Pallas kernels, read_pass(): pl.pallas_call(read_kernel, in_specs=resident(4), out_specs=resident(4),...  3.69 us
    pallas_call x1, Pallas kernels, finish(): pl.pallas_call(functools.partial(finish_kernel, owners), in_specs=residen...  1.37 us
    unnamed x7, local copies, waits for them, and re-layouts  0.77 us
  transfers between devices with their start and end apart: 6, of which 4 were waited for; matrix products, arithmetic and copies ran while one was open for 2% of the time, Pallas kernels for 10%

profile of v4, /device:TPU:0, one launch (start us, length us, event | category | flops | bytes accessed | tf_op | source)
XLA Modules:
  0.0 37.0 jit_solution(17113125670331439457)
XLA Ops:
  0.6 0.0 copy-start.1
  0.6 0.0 copy-start
  0.7 6.1 %range_pass.1 = (f32[5,64,128]{2,1,0:T(8,128)S(1)}, f32[5,64,128]{2,1,0:T(8,128)S(1)}, f32[5,64,128]{2,1,0:T(8,128)S(1)}, f32[5,64,128]{2,1,0:T(8,128)S(1)}, bf1...) custom-call(bf16[128,1280]{1,0:T(8,128)(2,1)} %bitcast.11, bf16[128,1280]{1,0:T(8,128)(2,1)} %bitcast.12, ...), custom_call_target="tpu_custom_call" | custom-call | tf_op jit(solution)/shard_map/range_pass/pallas_call | solution.py:297
  6.8 3.1 %collective-permute-start = (f32[5,64,128]{2,1,0:T(8,128)S(1)}, f32[5,64,128]{2,1,0:T(8,128)S(1)}, u32[]{:S(2)}, u32[]{:S(2)}) collective-permute-start(f32[5,64,128]{2,1,0:T(8,128)S(1)} %get-tuple-element.26), channel_id=1, source_target_pairs={{0,4},{4,8},{8,12},{12,0},{1,5},{5,9},{9,13},{13,1},{2,6},{6,10},{... | collective-permute-start | bytes 491528 | tf_op jit(solution)/shard_map/ppermute | solution.py:495
  9.9 2.6 %collective-permute-start.1 = (f32[5,64,128]{2,1,0:T(8,128)S(1)}, f32[5,64,128]{2,1,0:T(8,128)S(1)}, u32[]{:S(2)}, u32[]{:S(2)}) collective-permute-start(f32[5,64,128]{2,1,0:T(8,128)S(1)} %get-tuple-element.27), channel_id=1, source_target_pairs={{0,8},{4,12},{8,0},{12,4},{1,9},{5,13},{9,1},{13,5},{2,10},{6,14},... | collective-permute-start | bytes 491528 | tf_op jit(solution)/shard_map/ppermute | solution.py:495
  12.5 1.3 %collective-permute-start.2 = (f32[5,64,128]{2,1,0:T(8,128)S(1)}, f32[5,64,128]{2,1,0:T(8,128)S(1)}, u32[]{:S(2)}, u32[]{:S(2)}) collective-permute-start(f32[5,64,128]{2,1,0:T(8,128)S(1)} %get-tuple-element.28), channel_id=1, source_target_pairs={{0,12},{4,0},{8,4},{12,8},{1,13},{5,1},{9,5},{13,9},{2,14},{6,2},{... | collective-permute-start | bytes 491528 | tf_op jit(solution)/shard_map/ppermute | solution.py:495
  13.8 0.0 copy-done.1
  13.8 0.0 copy-done
  13.8 0.0 copy-start.2
  13.9 3.7 %read_pass.1 = (bf16[1280,128]{1,0:T(8,128)(2,1)S(1)}, bf16[1280,128]{1,0:T(8,128)(2,1)S(1)}, f32[1280,128]{1,0:T(8,128)S(1)}, f32[128,1280]{1,0:T(8,128)S(1)}) custom-call(bf16[128,1280]{1,0:T(8,128)(2,1)S(1)} %bitcast.8, f32[1,1280]{1,0:T(1,128)S(1)} %reshape.10.extra_ref, bf16[20,128,256]{2,1,0:T(8,128)(2,1)S(1)} %get-tuple-element.29.solved_ref, ...), custom_call_target="tpu_custom_call" | custom-call | tf_op jit(solution)/shard_map/read_pass/pallas_call | solution.py:373
  17.5 0.0 collective-permute-done.refs_1_
  17.6 5.7 %collective-permute-done.1.refs_2_ = f32[5,64,128]{2,1,0:T(8,128)S(1)} collective-permute-done((f32[5,64,128]{2,1,0:T(8,128)S(1)}, f32[5,64,128]{2,1,0:T(8,128)S(1)}, u32[]{:S(2)}, u32[]{:S(2)}) %collective-permute-start.1) | collective-permute-done | bytes 163872 | tf_op jit(solution)/shard_map/ppermute | solution.py:495
  23.2 0.0 collective-permute-done.2.refs_3_
  23.2 0.7 %chain.1 = (f32[5,32,128]{2,1,0:T(8,128)S(1)}, f32[5,32,128]{2,1,0:T(8,128)S(1)}, f32[5,32,128]{2,1,0:T(8,128)S(1)}, f32[5,32,128]{2,1,0:T(8,128)S(1)}, f32[320,64]{1,0:T(8,128)S(1)}) custom-call(f32[5,64,128]{2,1,0:T(8,128)S(1)} %get-tuple-element.35.refs_0_, f32[5,64,128]{2,1,0:T(8,128)S(1)} %collective-permute-done.refs_1_, ...), custom_call_target="tpu_custom_call" | custom-call | tf_op jit(solution)/shard_map/chain/pallas_call | solution.py:424
  24.0 4.0 %collective-permute-start.3 = (f32[5,32,128]{2,1,0:T(8,128)S(1)}, f32[5,32,128]{2,1,0:T(8,128)S(1)}, u32[]{:S(2)}, u32[]{:S(2)}) collective-permute-start(f32[5,32,128]{2,1,0:T(8,128)S(1)} %get-tuple-element.40), channel_id=1, source_target_pairs={{0,4},{4,8},{8,12},{12,0},{1,5},{5,9},{9,13},{13,1},{2,6},{6,10},{... | collective-permute-start | bytes 245768 | tf_op jit(solution)/shard_map/ppermute | solution.py:495
  28.0 1.6 %collective-permute-start.4 = (f32[5,32,128]{2,1,0:T(8,128)S(1)}, f32[5,32,128]{2,1,0:T(8,128)S(1)}, u32[]{:S(2)}, u32[]{:S(2)}) collective-permute-start(f32[5,32,128]{2,1,0:T(8,128)S(1)} %get-tuple-element.41), channel_id=1, source_target_pairs={{0,8},{4,12},{8,0},{12,4},{1,9},{5,13},{9,1},{13,5},{2,10},{6,14},... | collective-permute-start | bytes 245768 | tf_op jit(solution)/shard_map/ppermute | solution.py:495
  29.6 0.8 %collective-permute-start.5 = (f32[5,32,128]{2,1,0:T(8,128)S(1)}, f32[5,32,128]{2,1,0:T(8,128)S(1)}, u32[]{:S(2)}, u32[]{:S(2)}) collective-permute-start(f32[5,32,128]{2,1,0:T(8,128)S(1)} %get-tuple-element.42), channel_id=1, source_target_pairs={{0,12},{4,0},{8,4},{12,8},{1,13},{5,1},{9,5},{13,9},{2,14},{6,2},{... | collective-permute-start | bytes 245768 | tf_op jit(solution)/shard_map/ppermute | solution.py:495
  30.4 0.0 copy-done.2
  30.4 0.8 %copy.10 = f32[1,320,64]{1,2,0:T(8,128)} copy(f32[1,320,64]{2,1,0:T(8,128)S(1)} %bitcast.9) | data formatting | bytes 163840
  31.2 0.8 %collective-permute-done.3.refs_1_ = f32[5,32,128]{2,1,0:T(8,128)S(1)} collective-permute-done((f32[5,32,128]{2,1,0:T(8,128)S(1)}, f32[5,32,128]{2,1,0:T(8,128)S(1)}, u32[]{:S(2)}, u32[]{:S(2)}) %collective-permute-start.3) | collective-permute-done | bytes 81952 | tf_op jit(solution)/shard_map/ppermute | solution.py:495
  32.0 3.1 %collective-permute-done.4.refs_2_ = f32[5,32,128]{2,1,0:T(8,128)S(1)} collective-permute-done((f32[5,32,128]{2,1,0:T(8,128)S(1)}, f32[5,32,128]{2,1,0:T(8,128)S(1)}, u32[]{:S(2)}, u32[]{:S(2)}) %collective-permute-start.4) | collective-permute-done | bytes 81952 | tf_op jit(solution)/shard_map/ppermute | solution.py:495
  35.1 0.5 %collective-permute-done.5.refs_3_ = f32[5,32,128]{2,1,0:T(8,128)S(1)} collective-permute-done((f32[5,32,128]{2,1,0:T(8,128)S(1)}, f32[5,32,128]{2,1,0:T(8,128)S(1)}, u32[]{:S(2)}, u32[]{:S(2)}) %collective-permute-start.5) | collective-permute-done | bytes 81952 | tf_op jit(solution)/shard_map/ppermute | solution.py:495
  35.6 1.4 %finish.1 = bf16[128,1280]{1,0:T(8,128)(2,1)} custom-call(f32[5,32,128]{2,1,0:T(8,128)S(1)} %get-tuple-element.39.refs_0_, f32[5,32,128]{2,1,0:T(8,128)S(1)} %collective-permute-done.3.refs_1_, f32[5,32,128]{2,1,0:T(8,128)S(1)} %collective-permute-done.4.refs_2_, f32[5,32,128]{2,1,0:T(8,128)S(1)} %collective-permute-done.5.refs_3_, ...), custom_call_target="tpu_custom_call" | custom-call | tf_op jit(solution)/shard_map/finish/pallas_call | solution.py:483
  (2 shorter events, 0.0 us)
Async XLA Ops:
  0.6 13.2 %copy-start.1 = (f32[1280]{0:T(1024)S(1)}, f32[1280]{0:T(1024)}, u32[]{:S(2)}) copy-start(f32[1280]{0:T(1024)} %param.14) | copy-start | bytes 15364
  0.6 13.2 %copy-start = (bf16[1,128,1280]{2,1,0:T(8,128)(2,1)S(1)}, bf16[1,128,1280]{2,1,0:T(8,128)(2,1)}, u32[]{:S(2)}) copy-start(bf16[1,128,1280]{2,1,0:T(8,128)(2,1)} %param.8) | copy-start | bytes 983044
  6.8 10.8 %collective-permute-start = (f32[5,64,128]{2,1,0:T(8,128)S(1)}, f32[5,64,128]{2,1,0:T(8,128)S(1)}, u32[]{:S(2)}, u32[]{:S(2)}) collective-permute-start(f32[5,64,128]{2,1,0:T(8,128)S(1)} %get-tuple-element.26), channel_id=1, source_target_pairs={{0,4},{4,8},{8,12},{12,0},{1,5},{5,9},{9,13},{13,1},{2,6},{6,10},{... | collective-permute-start | bytes 491528 | tf_op jit(solution)/shard_map/ppermute | solution.py:495
  9.9 13.3 %collective-permute-start.1 = (f32[5,64,128]{2,1,0:T(8,128)S(1)}, f32[5,64,128]{2,1,0:T(8,128)S(1)}, u32[]{:S(2)}, u32[]{:S(2)}) collective-permute-start(f32[5,64,128]{2,1,0:T(8,128)S(1)} %get-tuple-element.27), channel_id=1, source_target_pairs={{0,8},{4,12},{8,0},{12,4},{1,9},{5,13},{9,1},{13,5},{2,10},{6,14},... | collective-permute-start | bytes 491528 | tf_op jit(solution)/shard_map/ppermute | solution.py:495
  12.5 10.7 %collective-permute-start.2 = (f32[5,64,128]{2,1,0:T(8,128)S(1)}, f32[5,64,128]{2,1,0:T(8,128)S(1)}, u32[]{:S(2)}, u32[]{:S(2)}) collective-permute-start(f32[5,64,128]{2,1,0:T(8,128)S(1)} %get-tuple-element.28), channel_id=1, source_target_pairs={{0,12},{4,0},{8,4},{12,8},{1,13},{5,1},{9,5},{13,9},{2,14},{6,2},{... | collective-permute-start | bytes 491528 | tf_op jit(solution)/shard_map/ppermute | solution.py:495
  13.8 16.6 %copy-start.2 = (f32[1280]{0:T(1024)S(1)}, f32[1280]{0:T(1024)}, u32[]{:S(2)}) copy-start(f32[1280]{0:T(1024)} %param.15) | copy-start | bytes 15364
  24.0 8.1 %collective-permute-start.3 = (f32[5,32,128]{2,1,0:T(8,128)S(1)}, f32[5,32,128]{2,1,0:T(8,128)S(1)}, u32[]{:S(2)}, u32[]{:S(2)}) collective-permute-start(f32[5,32,128]{2,1,0:T(8,128)S(1)} %get-tuple-element.40), channel_id=1, source_target_pairs={{0,4},{4,8},{8,12},{12,0},{1,5},{5,9},{9,13},{13,1},{2,6},{6,10},{... | collective-permute-start | bytes 245768 | tf_op jit(solution)/shard_map/ppermute | solution.py:495
  28.0 7.1 %collective-permute-start.4 = (f32[5,32,128]{2,1,0:T(8,128)S(1)}, f32[5,32,128]{2,1,0:T(8,128)S(1)}, u32[]{:S(2)}, u32[]{:S(2)}) collective-permute-start(f32[5,32,128]{2,1,0:T(8,128)S(1)} %get-tuple-element.41), channel_id=1, source_target_pairs={{0,8},{4,12},{8,0},{12,4},{1,9},{5,13},{9,1},{13,5},{2,10},{6,14},... | collective-permute-start | bytes 245768 | tf_op jit(solution)/shard_map/ppermute | solution.py:495
  29.6 6.0 %collective-permute-start.5 = (f32[5,32,128]{2,1,0:T(8,128)S(1)}, f32[5,32,128]{2,1,0:T(8,128)S(1)}, u32[]{:S(2)}, u32[]{:S(2)}) collective-permute-start(f32[5,32,128]{2,1,0:T(8,128)S(1)} %get-tuple-element.42), channel_id=1, source_target_pairs={{0,12},{4,0},{8,4},{12,8},{1,13},{5,1},{9,5},{13,9},{2,14},{6,2},{... | collective-permute-start | bytes 245768 | tf_op jit(solution)/shard_map/ppermute | solution.py:495

commit v5 on v4

--- a/solution.py
+++ b/solution.py
@@ -77,14 +77,7 @@
 
 
 def lane_blocks(x, low, high):
-    parts = []
-    for i in range(2):
-        one = x[:, i * PAIR : (i + 1) * PAIR]
-        none = jnp.zeros_like(one)
-        for mask in (low, high):
-            kept = one * mask
-            parts.append(side(kept, none) if i == 0 else side(none, kept))
-    return stack(*parts)
+    return stack(x * low, x * high)
 
 
 def scores(late, away, keys, query, terms):
@@ -167,10 +160,10 @@
     toward_abs = toward_mid * jnp.exp(middle)
 
     cuts = [slice(p * PAIR, (p + 1) * PAIR) for p in range(pairs)]
-    block = iota((d, 2 * PAIR), 1) % PAIR
+    block = iota((d, PAIR), 1)
     is_low = block < d
-    strict = iota((d, 2 * PAIR), 0) < block % d
-    unit = iota((d, 2 * PAIR), 0) == block % d
+    strict = iota((d, PAIR), 0) < block % d
+    unit = iota((d, PAIR), 0) == block % d
     low = (iota((d, PAIR), 1) < d).astype(F32).astype(BF16)
     high = (iota((d, PAIR), 1) >= d).astype(F32).astype(BF16)
 
@@ -199,48 +192,48 @@
     ]
     mixes = []
     for early, later in scored:
-        mix_early, mix_later = early[:d], later[:d]
-        power = jnp.where(strict, jnp.where(is_low, mix_early, mix_later), 0.0)
-        inverses.append(jnp.where(unit, 1.0, power))
-        powers.append(power.astype(BF16))
-        across.append(jnp.where(is_low, 0.0, mix_early))
-        key_early = jnp.where(is_low & ~strict, 0.0, early[d:])
-        key_later = jnp.where(~is_low & strict, later[d:], 0.0)
-        mixes.append(stack(key_early.astype(BF16), key_later.astype(BF16)))
-    none = jnp.zeros((tokens, tokens), BF16)
-    for both, mixed in zip(turned, mixes):
-        start, value_t = both[:, :tokens], both[:, tokens:].astype(BF16)
-        mixed = stack(side(mixed[:, :tokens], none), side(none, mixed[:, tokens:]))
-        moved = mm(side(value_t[:d], value_t[d:]), mixed)
-        known.append(stack(side(start[:d], start[d:]), moved))
-        values.append(value_t)
-
+        for i in range(2):
+            mine = slice(i * tokens, (i + 1) * tokens)
+            one, two = early[:, mine], later[:, mine]
+            power = jnp.where(strict, jnp.where(is_low, one[:d], two[:d]), 0.0)
+            inverses.append(jnp.where(unit, 1.0, power))
+            powers.append(power.astype(BF16))
+            across.append(jnp.where(is_low, 0.0, one[:d]))
+            key_early = jnp.where(is_low & ~strict, 0.0, one[d:])
+            key_later = jnp.where(~is_low & strict, two[d:], 0.0)
+            mixes.append(stack(key_early.astype(BF16), key_later.astype(BF16)))
+    for both in turned:
+        for i in range(2):
+            mine = slice(i * d, (i + 1) * d)
+            value_h = both[mine, tokens:].astype(BF16)
+            moved = mm(value_h, mixes[len(known)])
+            known.append(stack(both[mine, :tokens], moved))
+            values.append(value_h)
+
+    count = 2 * pairs
     reach = 1
     while reach < d:
-        for p in range(pairs):
-            factor = lane_blocks(powers[p], low, high)
+        for h in range(count):
+            factor = lane_blocks(powers[h], low, high)
             if reach == 1:
-                powers[p] = mm(powers[p], factor).astype(BF16)
+                powers[h] = mm(powers[h], factor).astype(BF16)
             elif reach * 2 < d:
-                out = mm(stack(inverses[p].astype(BF16), powers[p]), factor)
-                inverses[p] = inverses[p] + out[:d]
-                powers[p] = out[d:].astype(BF16)
+                out = mm(stack(inverses[h].astype(BF16), powers[h]), factor)
+                inverses[h] = inverses[h] + out[:d]
+                powers[h] = out[d:].astype(BF16)
             else:
-                inverses[p] = inverses[p] + mm(inverses[p].astype(BF16), factor)
+                inverses[h] = inverses[h] + mm(inverses[h].astype(BF16), factor)
         reach *= 2
+    for h in range(count):
+        rest = jnp.where(strict, inverses[h], 0.0).astype(BF16)
+        left = stack(known[h].astype(BF16), across[h].astype(BF16))
+        out = mm(left, lane_blocks(rest, low, high))
+        known[h] = known[h] + out[:tokens]
+        across[h] = (across[h] + out[tokens:]).astype(BF16)
     solved = []
-    for p in range(pairs):
-        rest = jnp.where(strict, inverses[p], 0.0).astype(BF16)
-        factor = lane_blocks(rest, low, high)
-        left = stack(known[p].astype(BF16), across[p].astype(BF16))
-        out = mm(left, factor)
-        solved.append(known[p] + out[:tokens])
-        across[p] = (across[p] + out[tokens:]).astype(BF16)
-    for p in range(pairs):
-        one, two = across[p][:, :PAIR], across[p][:, PAIR:]
-        none = jnp.zeros_like(one)
-        factor = stack(side(one, none), side(none, none), side(none, two), side(none, none))
-        solved[p] = (solved[p] + mm(solved[p].astype(BF16), factor)).astype(BF16)
+    for h in range(count):
+        factor = stack(across[h], jnp.zeros_like(across[h]))
+        solved.append((known[h] + mm(known[h].astype(BF16), factor)).astype(BF16))
 
     lane = iota((d, PAIR), 1)
     sub = iota((d, PAIR), 0)
@@ -250,10 +243,7 @@
         away_end = side(away_end, jnp.zeros_like(away_end))
         keys_end = side(*split(keys[:, cut] * to_end[:, cut]))
         lefts = [
-            side(
-                solved[p][:, i * tokens : (i + 1) * tokens],
-                stack(none, values[p][i * d : (i + 1) * d]),
-            )
+            side(solved[2 * p + i], stack(none, values[2 * p + i]))
             for i in range(2)
         ]
         ended = folded(stack(*lefts), stack(away_end, keys_end))

time: 37.1 us -> 36.9 us (level)
  no operation moved by 1% of the time
where the time goes in v5:
time: 36.9 us; the launch traced here: 36.8 us
  starting transfers between devices  13.5 us (37%)
  Pallas kernels  11.7 us (32%)
  waiting for transfers between devices  10.1 us (27%)
  local copies, waits for them, and re-layouts  0.78 us (2%)
  between operations  0.7 us (2%)
    ppermute x6, starting transfers between devices, shifted(): lax.ppermute(value, 'seq', [(i, (i + by) % members) for i in range(member...  13.5 us
    ppermute x6, waiting for transfers between devices, shifted(): lax.ppermute(value, 'seq', [(i, (i + by) % members) for i in range(member...  10.1 us
    pallas_call x1, Pallas kernels, range_pass(): pl.pallas_call(functools.partial(range_kernel, owners), in_specs=[pl.Bloc...  5.91 us
    pallas_call x1, Pallas kernels, read_pass(): pl.pallas_call(read_kernel, in_specs=resident(4), out_specs=resident(4),...  3.68 us
    pallas_call x1, Pallas kernels, finish(): pl.pallas_call(functools.partial(finish_kernel, owners), in_specs=residen...  1.37 us
    unnamed x7, local copies, waits for them, and re-layouts  0.77 us
  transfers between devices with their start and end apart: 6, of which 4 were waited for; matrix products, arithmetic and copies ran while one was open for 2% of the time, Pallas kernels for 10%

profile of v5, /device:TPU:0, one launch (start us, length us, event | category | flops | bytes accessed | tf_op | source)
XLA Modules:
  0.0 36.8 jit_solution(6394366169884198780)
XLA Ops:
  0.6 0.0 copy-start.1
  0.6 0.0 copy-start
  0.7 5.9 %range_pass.1 = (f32[5,64,128]{2,1,0:T(8,128)S(1)}, f32[5,64,128]{2,1,0:T(8,128)S(1)}, f32[5,64,128]{2,1,0:T(8,128)S(1)}, f32[5,64,128]{2,1,0:T(8,128)S(1)}, bf1...) custom-call(bf16[128,1280]{1,0:T(8,128)(2,1)} %bitcast.11, bf16[128,1280]{1,0:T(8,128)(2,1)} %bitcast.12, ...), custom_call_target="tpu_custom_call" | custom-call | tf_op jit(solution)/shard_map/range_pass/pallas_call | solution.py:287
  6.6 3.1 %collective-permute-start = (f32[5,64,128]{2,1,0:T(8,128)S(1)}, f32[5,64,128]{2,1,0:T(8,128)S(1)}, u32[]{:S(2)}, u32[]{:S(2)}) collective-permute-start(f32[5,64,128]{2,1,0:T(8,128)S(1)} %get-tuple-element.26), channel_id=1, source_target_pairs={{0,4},{4,8},{8,12},{12,0},{1,5},{5,9},{9,13},{13,1},{2,6},{6,10},{... | collective-permute-start | bytes 491528 | tf_op jit(solution)/shard_map/ppermute | solution.py:485
  9.7 2.6 %collective-permute-start.1 = (f32[5,64,128]{2,1,0:T(8,128)S(1)}, f32[5,64,128]{2,1,0:T(8,128)S(1)}, u32[]{:S(2)}, u32[]{:S(2)}) collective-permute-start(f32[5,64,128]{2,1,0:T(8,128)S(1)} %get-tuple-element.27), channel_id=1, source_target_pairs={{0,8},{4,12},{8,0},{12,4},{1,9},{5,13},{9,1},{13,5},{2,10},{6,14},... | collective-permute-start | bytes 491528 | tf_op jit(solution)/shard_map/ppermute | solution.py:485
  12.3 1.3 %collective-permute-start.2 = (f32[5,64,128]{2,1,0:T(8,128)S(1)}, f32[5,64,128]{2,1,0:T(8,128)S(1)}, u32[]{:S(2)}, u32[]{:S(2)}) collective-permute-start(f32[5,64,128]{2,1,0:T(8,128)S(1)} %get-tuple-element.28), channel_id=1, source_target_pairs={{0,12},{4,0},{8,4},{12,8},{1,13},{5,1},{9,5},{13,9},{2,14},{6,2},{... | collective-permute-start | bytes 491528 | tf_op jit(solution)/shard_map/ppermute | solution.py:485
  13.6 0.0 copy-done.1
  13.6 0.0 copy-done
  13.6 0.0 copy-start.2
  13.6 3.7 %read_pass.1 = (bf16[1280,128]{1,0:T(8,128)(2,1)S(1)}, bf16[1280,128]{1,0:T(8,128)(2,1)S(1)}, f32[1280,128]{1,0:T(8,128)S(1)}, f32[128,1280]{1,0:T(8,128)S(1)}) custom-call(bf16[128,1280]{1,0:T(8,128)(2,1)S(1)} %bitcast.8, f32[1,1280]{1,0:T(1,128)S(1)} %reshape.10.extra_ref, bf16[20,128,256]{2,1,0:T(8,128)(2,1)S(1)} %get-tuple-element.29.solved_ref, ...), custom_call_target="tpu_custom_call" | custom-call | tf_op jit(solution)/shard_map/read_pass/pallas_call | solution.py:363
  17.3 0.0 collective-permute-done.refs_1_
  17.3 5.7 %collective-permute-done.1.refs_2_ = f32[5,64,128]{2,1,0:T(8,128)S(1)} collective-permute-done((f32[5,64,128]{2,1,0:T(8,128)S(1)}, f32[5,64,128]{2,1,0:T(8,128)S(1)}, u32[]{:S(2)}, u32[]{:S(2)}) %collective-permute-start.1) | collective-permute-done | bytes 163872 | tf_op jit(solution)/shard_map/ppermute | solution.py:485
  23.0 0.0 collective-permute-done.2.refs_3_
  23.0 0.7 %chain.1 = (f32[5,32,128]{2,1,0:T(8,128)S(1)}, f32[5,32,128]{2,1,0:T(8,128)S(1)}, f32[5,32,128]{2,1,0:T(8,128)S(1)}, f32[5,32,128]{2,1,0:T(8,128)S(1)}, f32[320,64]{1,0:T(8,128)S(1)}) custom-call(f32[5,64,128]{2,1,0:T(8,128)S(1)} %get-tuple-element.35.refs_0_, f32[5,64,128]{2,1,0:T(8,128)S(1)} %collective-permute-done.refs_1_, ...), custom_call_target="tpu_custom_call" | custom-call | tf_op jit(solution)/shard_map/chain/pallas_call | solution.py:414
  23.8 4.0 %collective-permute-start.3 = (f32[5,32,128]{2,1,0:T(8,128)S(1)}, f32[5,32,128]{2,1,0:T(8,128)S(1)}, u32[]{:S(2)}, u32[]{:S(2)}) collective-permute-start(f32[5,32,128]{2,1,0:T(8,128)S(1)} %get-tuple-element.40), channel_id=1, source_target_pairs={{0,4},{4,8},{8,12},{12,0},{1,5},{5,9},{9,13},{13,1},{2,6},{6,10},{... | collective-permute-start | bytes 245768 | tf_op jit(solution)/shard_map/ppermute | solution.py:485
  27.8 1.6 %collective-permute-start.4 = (f32[5,32,128]{2,1,0:T(8,128)S(1)}, f32[5,32,128]{2,1,0:T(8,128)S(1)}, u32[]{:S(2)}, u32[]{:S(2)}) collective-permute-start(f32[5,32,128]{2,1,0:T(8,128)S(1)} %get-tuple-element.41), channel_id=1, source_target_pairs={{0,8},{4,12},{8,0},{12,4},{1,9},{5,13},{9,1},{13,5},{2,10},{6,14},... | collective-permute-start | bytes 245768 | tf_op jit(solution)/shard_map/ppermute | solution.py:485
  29.4 0.8 %collective-permute-start.5 = (f32[5,32,128]{2,1,0:T(8,128)S(1)}, f32[5,32,128]{2,1,0:T(8,128)S(1)}, u32[]{:S(2)}, u32[]{:S(2)}) collective-permute-start(f32[5,32,128]{2,1,0:T(8,128)S(1)} %get-tuple-element.42), channel_id=1, source_target_pairs={{0,12},{4,0},{8,4},{12,8},{1,13},{5,1},{9,5},{13,9},{2,14},{6,2},{... | collective-permute-start | bytes 245768 | tf_op jit(solution)/shard_map/ppermute | solution.py:485
  30.2 0.0 copy-done.2
  30.2 0.8 %copy.10 = f32[1,320,64]{1,2,0:T(8,128)} copy(f32[1,320,64]{2,1,0:T(8,128)S(1)} %bitcast.9) | data formatting | bytes 163840
  31.0 0.8 %collective-permute-done.3.refs_1_ = f32[5,32,128]{2,1,0:T(8,128)S(1)} collective-permute-done((f32[5,32,128]{2,1,0:T(8,128)S(1)}, f32[5,32,128]{2,1,0:T(8,128)S(1)}, u32[]{:S(2)}, u32[]{:S(2)}) %collective-permute-start.3) | collective-permute-done | bytes 81952 | tf_op jit(solution)/shard_map/ppermute | solution.py:485
  31.8 3.1 %collective-permute-done.4.refs_2_ = f32[5,32,128]{2,1,0:T(8,128)S(1)} collective-permute-done((f32[5,32,128]{2,1,0:T(8,128)S(1)}, f32[5,32,128]{2,1,0:T(8,128)S(1)}, u32[]{:S(2)}, u32[]{:S(2)}) %collective-permute-start.4) | collective-permute-done | bytes 81952 | tf_op jit(solution)/shard_map/ppermute | solution.py:485
  34.9 0.5 %collective-permute-done.5.refs_3_ = f32[5,32,128]{2,1,0:T(8,128)S(1)} collective-permute-done((f32[5,32,128]{2,1,0:T(8,128)S(1)}, f32[5,32,128]{2,1,0:T(8,128)S(1)}, u32[]{:S(2)}, u32[]{:S(2)}) %collective-permute-start.5) | collective-permute-done | bytes 81952 | tf_op jit(solution)/shard_map/ppermute | solution.py:485
  35.4 1.4 %finish.1 = bf16[128,1280]{1,0:T(8,128)(2,1)} custom-call(f32[5,32,128]{2,1,0:T(8,128)S(1)} %get-tuple-element.39.refs_0_, f32[5,32,128]{2,1,0:T(8,128)S(1)} %collective-permute-done.3.refs_1_, f32[5,32,128]{2,1,0:T(8,128)S(1)} %collective-permute-done.4.refs_2_, f32[5,32,128]{2,1,0:T(8,128)S(1)} %collective-permute-done.5.refs_3_, ...), custom_call_target="tpu_custom_call" | custom-call | tf_op jit(solution)/shard_map/finish/pallas_call | solution.py:473
  (2 shorter events, 0.0 us)
Async XLA Ops:
  0.6 13.0 %copy-start.1 = (f32[1280]{0:T(1024)S(1)}, f32[1280]{0:T(1024)}, u32[]{:S(2)}) copy-start(f32[1280]{0:T(1024)} %param.14) | copy-start | bytes 15364
  0.6 13.0 %copy-start = (bf16[1,128,1280]{2,1,0:T(8,128)(2,1)S(1)}, bf16[1,128,1280]{2,1,0:T(8,128)(2,1)}, u32[]{:S(2)}) copy-start(bf16[1,128,1280]{2,1,0:T(8,128)(2,1)} %param.8) | copy-start | bytes 983044
  6.6 10.8 %collective-permute-start = (f32[5,64,128]{2,1,0:T(8,128)S(1)}, f32[5,64,128]{2,1,0:T(8,128)S(1)}, u32[]{:S(2)}, u32[]{:S(2)}) collective-permute-start(f32[5,64,128]{2,1,0:T(8,128)S(1)} %get-tuple-element.26), channel_id=1, source_target_pairs={{0,4},{4,8},{8,12},{12,0},{1,5},{5,9},{9,13},{13,1},{2,6},{6,10},{... | collective-permute-start | bytes 491528 | tf_op jit(solution)/shard_map/ppermute | solution.py:485
  9.7 13.3 %collective-permute-start.1 = (f32[5,64,128]{2,1,0:T(8,128)S(1)}, f32[5,64,128]{2,1,0:T(8,128)S(1)}, u32[]{:S(2)}, u32[]{:S(2)}) collective-permute-start(f32[5,64,128]{2,1,0:T(8,128)S(1)} %get-tuple-element.27), channel_id=1, source_target_pairs={{0,8},{4,12},{8,0},{12,4},{1,9},{5,13},{9,1},{13,5},{2,10},{6,14},... | collective-permute-start | bytes 491528 | tf_op jit(solution)/shard_map/ppermute | solution.py:485
  12.3 10.7 %collective-permute-start.2 = (f32[5,64,128]{2,1,0:T(8,128)S(1)}, f32[5,64,128]{2,1,0:T(8,128)S(1)}, u32[]{:S(2)}, u32[]{:S(2)}) collective-permute-start(f32[5,64,128]{2,1,0:T(8,128)S(1)} %get-tuple-element.28), channel_id=1, source_target_pairs={{0,12},{4,0},{8,4},{12,8},{1,13},{5,1},{9,5},{13,9},{2,14},{6,2},{... | collective-permute-start | bytes 491528 | tf_op jit(solution)/shard_map/ppermute | solution.py:485
  13.6 16.6 %copy-start.2 = (f32[1280]{0:T(1024)S(1)}, f32[1280]{0:T(1024)}, u32[]{:S(2)}) copy-start(f32[1280]{0:T(1024)} %param.15) | copy-start | bytes 15364
  23.8 8.1 %collective-permute-start.3 = (f32[5,32,128]{2,1,0:T(8,128)S(1)}, f32[5,32,128]{2,1,0:T(8,128)S(1)}, u32[]{:S(2)}, u32[]{:S(2)}) collective-permute-start(f32[5,32,128]{2,1,0:T(8,128)S(1)} %get-tuple-element.40), channel_id=1, source_target_pairs={{0,4},{4,8},{8,12},{12,0},{1,5},{5,9},{9,13},{13,1},{2,6},{6,10},{... | collective-permute-start | bytes 245768 | tf_op jit(solution)/shard_map/ppermute | solution.py:485
  27.8 7.1 %collective-permute-start.4 = (f32[5,32,128]{2,1,0:T(8,128)S(1)}, f32[5,32,128]{2,1,0:T(8,128)S(1)}, u32[]{:S(2)}, u32[]{:S(2)}) collective-permute-start(f32[5,32,128]{2,1,0:T(8,128)S(1)} %get-tuple-element.41), channel_id=1, source_target_pairs={{0,8},{4,12},{8,0},{12,4},{1,9},{5,13},{9,1},{13,5},{2,10},{6,14},... | collective-permute-start | bytes 245768 | tf_op jit(solution)/shard_map/ppermute | solution.py:485
  29.4 6.0 %collective-permute-start.5 = (f32[5,32,128]{2,1,0:T(8,128)S(1)}, f32[5,32,128]{2,1,0:T(8,128)S(1)}, u32[]{:S(2)}, u32[]{:S(2)}) collective-permute-start(f32[5,32,128]{2,1,0:T(8,128)S(1)} %get-tuple-element.42), channel_id=1, source_target_pairs={{0,12},{4,0},{8,4},{12,8},{1,13},{5,1},{9,5},{13,9},{2,14},{6,2},{... | collective-permute-start | bytes 245768 | tf_op jit(solution)/shard_map/ppermute | solution.py:485

commit v6 on v5

--- a/solution.py
+++ b/solution.py
@@ -442,22 +442,20 @@
         states[lax.rem(me % owners - k + owners, owners)] = state_refs[k][...]
 
     lane = iota((d // 2, PAIR), 1)
+    results = []
+    for head in range(width // d):
+        packed = states[head // per_owner, head % per_owner]
+        state = split(
+            stack(jnp.where(lane < d, packed, 0.0), jnp.where(lane >= d, packed, 0.0))
+        )
+        at = slice(head * d, (head + 1) * d)
+        high, low = lift_high_ref[at], lift_low_ref[at]
+        results.append(
+            within_ref[at] + mm3(state, (stack(high, high), stack(low, low)))
+        )
     for p in range(width // PAIR):
         normed = []
-        for i in range(2):
-            head = 2 * p + i
-            packed = states[head // per_owner, head % per_owner]
-            state = split(
-                stack(
-                    jnp.where(lane < d, packed, 0.0),
-                    jnp.where(lane >= d, packed, 0.0),
-                )
-            )
-            at = slice(p * PAIR + i * d, p * PAIR + (i + 1) * d)
-            high, low = lift_high_ref[at], lift_low_ref[at]
-            result = within_ref[at] + mm3(
-                state, (stack(high, high), stack(low, low))
-            )
+        for result in results[2 * p : 2 * p + 2]:
             average = jnp.mean(result, axis=0, keepdims=True)
             centered = result - average
             spread = jnp.mean(centered * centered, axis=0, keepdims=True)

time: 36.9 us -> 36.9 us (level)
  no operation moved by 1% of the time
where the time goes in v6:
time: 36.9 us; the launch traced here: 36.8 us
  starting transfers between devices  13.5 us (37%)
  Pallas kernels  11.7 us (32%)
  waiting for transfers between devices  10.1 us (27%)
  local copies, waits for them, and re-layouts  0.78 us (2%)
  between operations  0.7 us (2%)
    ppermute x6, starting transfers between devices, shifted(): lax.ppermute(value, 'seq', [(i, (i + by) % members) for i in range(member...  13.5 us
    ppermute x6, waiting for transfers between devices, shifted(): lax.ppermute(value, 'seq', [(i, (i + by) % members) for i in range(member...  10.1 us
    pallas_call x1, Pallas kernels, range_pass(): pl.pallas_call(functools.partial(range_kernel, owners), in_specs=[pl.Bloc...  5.91 us
    pallas_call x1, Pallas kernels, read_pass(): pl.pallas_call(read_kernel, in_specs=resident(4), out_specs=resident(4),...  3.68 us
    pallas_call x1, Pallas kernels, finish(): pl.pallas_call(functools.partial(finish_kernel, owners), in_specs=residen...  1.37 us
    unnamed x7, local copies, waits for them, and re-layouts  0.77 us
  transfers between devices with their start and end apart: 6, of which 4 were waited for; matrix products, arithmetic and copies ran while one was open for 2% of the time, Pallas kernels for 10%

profile of v6, /device:TPU:0, one launch (start us, length us, event | category | flops | bytes accessed | tf_op | source)
XLA Modules:
  0.0 36.8 jit_solution(6394366169884198780)
XLA Ops:
  0.6 0.0 copy-start.1
  0.6 0.0 copy-start
  0.7 5.9 %range_pass.1 = (f32[5,64,128]{2,1,0:T(8,128)S(1)}, f32[5,64,128]{2,1,0:T(8,128)S(1)}, f32[5,64,128]{2,1,0:T(8,128)S(1)}, f32[5,64,128]{2,1,0:T(8,128)S(1)}, bf1...) custom-call(bf16[128,1280]{1,0:T(8,128)(2,1)} %bitcast.11, bf16[128,1280]{1,0:T(8,128)(2,1)} %bitcast.12, ...), custom_call_target="tpu_custom_call" | custom-call | tf_op jit(solution)/shard_map/range_pass/pallas_call | solution.py:287
  6.6 3.1 %collective-permute-start = (f32[5,64,128]{2,1,0:T(8,128)S(1)}, f32[5,64,128]{2,1,0:T(8,128)S(1)}, u32[]{:S(2)}, u32[]{:S(2)}) collective-permute-start(f32[5,64,128]{2,1,0:T(8,128)S(1)} %get-tuple-element.26), channel_id=1, source_target_pairs={{0,4},{4,8},{8,12},{12,0},{1,5},{5,9},{9,13},{13,1},{2,6},{6,10},{... | collective-permute-start | bytes 491528 | tf_op jit(solution)/shard_map/ppermute | solution.py:483
  9.7 2.6 %collective-permute-start.1 = (f32[5,64,128]{2,1,0:T(8,128)S(1)}, f32[5,64,128]{2,1,0:T(8,128)S(1)}, u32[]{:S(2)}, u32[]{:S(2)}) collective-permute-start(f32[5,64,128]{2,1,0:T(8,128)S(1)} %get-tuple-element.27), channel_id=1, source_target_pairs={{0,8},{4,12},{8,0},{12,4},{1,9},{5,13},{9,1},{13,5},{2,10},{6,14},... | collective-permute-start | bytes 491528 | tf_op jit(solution)/shard_map/ppermute | solution.py:483
  12.3 1.3 %collective-permute-start.2 = (f32[5,64,128]{2,1,0:T(8,128)S(1)}, f32[5,64,128]{2,1,0:T(8,128)S(1)}, u32[]{:S(2)}, u32[]{:S(2)}) collective-permute-start(f32[5,64,128]{2,1,0:T(8,128)S(1)} %get-tuple-element.28), channel_id=1, source_target_pairs={{0,12},{4,0},{8,4},{12,8},{1,13},{5,1},{9,5},{13,9},{2,14},{6,2},{... | collective-permute-start | bytes 491528 | tf_op jit(solution)/shard_map/ppermute | solution.py:483
  13.6 0.0 copy-done.1
  13.6 0.0 copy-done
  13.6 0.0 copy-start.2
  13.6 3.7 %read_pass.1 = (bf16[1280,128]{1,0:T(8,128)(2,1)S(1)}, bf16[1280,128]{1,0:T(8,128)(2,1)S(1)}, f32[1280,128]{1,0:T(8,128)S(1)}, f32[128,1280]{1,0:T(8,128)S(1)}) custom-call(bf16[128,1280]{1,0:T(8,128)(2,1)S(1)} %bitcast.8, f32[1,1280]{1,0:T(1,128)S(1)} %reshape.10.extra_ref, bf16[20,128,256]{2,1,0:T(8,128)(2,1)S(1)} %get-tuple-element.29.solved_ref, ...), custom_call_target="tpu_custom_call" | custom-call | tf_op jit(solution)/shard_map/read_pass/pallas_call | solution.py:363
  17.3 0.0 collective-permute-done.refs_1_
  17.3 5.7 %collective-permute-done.1.refs_2_ = f32[5,64,128]{2,1,0:T(8,128)S(1)} collective-permute-done((f32[5,64,128]{2,1,0:T(8,128)S(1)}, f32[5,64,128]{2,1,0:T(8,128)S(1)}, u32[]{:S(2)}, u32[]{:S(2)}) %collective-permute-start.1) | collective-permute-done | bytes 163872 | tf_op jit(solution)/shard_map/ppermute | solution.py:483
  23.0 0.0 collective-permute-done.2.refs_3_
  23.0 0.7 %chain.1 = (f32[5,32,128]{2,1,0:T(8,128)S(1)}, f32[5,32,128]{2,1,0:T(8,128)S(1)}, f32[5,32,128]{2,1,0:T(8,128)S(1)}, f32[5,32,128]{2,1,0:T(8,128)S(1)}, f32[320,64]{1,0:T(8,128)S(1)}) custom-call(f32[5,64,128]{2,1,0:T(8,128)S(1)} %get-tuple-element.35.refs_0_, f32[5,64,128]{2,1,0:T(8,128)S(1)} %collective-permute-done.refs_1_, ...), custom_call_target="tpu_custom_call" | custom-call | tf_op jit(solution)/shard_map/chain/pallas_call | solution.py:414
  23.8 4.0 %collective-permute-start.3 = (f32[5,32,128]{2,1,0:T(8,128)S(1)}, f32[5,32,128]{2,1,0:T(8,128)S(1)}, u32[]{:S(2)}, u32[]{:S(2)}) collective-permute-start(f32[5,32,128]{2,1,0:T(8,128)S(1)} %get-tuple-element.40), channel_id=1, source_target_pairs={{0,4},{4,8},{8,12},{12,0},{1,5},{5,9},{9,13},{13,1},{2,6},{6,10},{... | collective-permute-start | bytes 245768 | tf_op jit(solution)/shard_map/ppermute | solution.py:483
  27.8 1.6 %collective-permute-start.4 = (f32[5,32,128]{2,1,0:T(8,128)S(1)}, f32[5,32,128]{2,1,0:T(8,128)S(1)}, u32[]{:S(2)}, u32[]{:S(2)}) collective-permute-start(f32[5,32,128]{2,1,0:T(8,128)S(1)} %get-tuple-element.41), channel_id=1, source_target_pairs={{0,8},{4,12},{8,0},{12,4},{1,9},{5,13},{9,1},{13,5},{2,10},{6,14},... | collective-permute-start | bytes 245768 | tf_op jit(solution)/shard_map/ppermute | solution.py:483
  29.4 0.8 %collective-permute-start.5 = (f32[5,32,128]{2,1,0:T(8,128)S(1)}, f32[5,32,128]{2,1,0:T(8,128)S(1)}, u32[]{:S(2)}, u32[]{:S(2)}) collective-permute-start(f32[5,32,128]{2,1,0:T(8,128)S(1)} %get-tuple-element.42), channel_id=1, source_target_pairs={{0,12},{4,0},{8,4},{12,8},{1,13},{5,1},{9,5},{13,9},{2,14},{6,2},{... | collective-permute-start | bytes 245768 | tf_op jit(solution)/shard_map/ppermute | solution.py:483
  30.2 0.0 copy-done.2
  30.2 0.8 %copy.10 = f32[1,320,64]{1,2,0:T(8,128)} copy(f32[1,320,64]{2,1,0:T(8,128)S(1)} %bitcast.9) | data formatting | bytes 163840
  31.0 0.8 %collective-permute-done.3.refs_1_ = f32[5,32,128]{2,1,0:T(8,128)S(1)} collective-permute-done((f32[5,32,128]{2,1,0:T(8,128)S(1)}, f32[5,32,128]{2,1,0:T(8,128)S(1)}, u32[]{:S(2)}, u32[]{:S(2)}) %collective-permute-start.3) | collective-permute-done | bytes 81952 | tf_op jit(solution)/shard_map/ppermute | solution.py:483
  31.8 3.1 %collective-permute-done.4.refs_2_ = f32[5,32,128]{2,1,0:T(8,128)S(1)} collective-permute-done((f32[5,32,128]{2,1,0:T(8,128)S(1)}, f32[5,32,128]{2,1,0:T(8,128)S(1)}, u32[]{:S(2)}, u32[]{:S(2)}) %collective-permute-start.4) | collective-permute-done | bytes 81952 | tf_op jit(solution)/shard_map/ppermute | solution.py:483
  34.9 0.5 %collective-permute-done.5.refs_3_ = f32[5,32,128]{2,1,0:T(8,128)S(1)} collective-permute-done((f32[5,32,128]{2,1,0:T(8,128)S(1)}, f32[5,32,128]{2,1,0:T(8,128)S(1)}, u32[]{:S(2)}, u32[]{:S(2)}) %collective-permute-start.5) | collective-permute-done | bytes 81952 | tf_op jit(solution)/shard_map/ppermute | solution.py:483
  35.4 1.4 %finish.1 = bf16[128,1280]{1,0:T(8,128)(2,1)} custom-call(f32[5,32,128]{2,1,0:T(8,128)S(1)} %get-tuple-element.39.refs_0_, f32[5,32,128]{2,1,0:T(8,128)S(1)} %collective-permute-done.3.refs_1_, f32[5,32,128]{2,1,0:T(8,128)S(1)} %collective-permute-done.4.refs_2_, f32[5,32,128]{2,1,0:T(8,128)S(1)} %collective-permute-done.5.refs_3_, ...), custom_call_target="tpu_custom_call" | custom-call | tf_op jit(solution)/shard_map/finish/pallas_call | solution.py:471
  (2 shorter events, 0.0 us)
Async XLA Ops:
  0.6 13.0 %copy-start.1 = (f32[1280]{0:T(1024)S(1)}, f32[1280]{0:T(1024)}, u32[]{:S(2)}) copy-start(f32[1280]{0:T(1024)} %param.14) | copy-start | bytes 15364
  0.6 13.0 %copy-start = (bf16[1,128,1280]{2,1,0:T(8,128)(2,1)S(1)}, bf16[1,128,1280]{2,1,0:T(8,128)(2,1)}, u32[]{:S(2)}) copy-start(bf16[1,128,1280]{2,1,0:T(8,128)(2,1)} %param.8) | copy-start | bytes 983044
  6.6 10.8 %collective-permute-start = (f32[5,64,128]{2,1,0:T(8,128)S(1)}, f32[5,64,128]{2,1,0:T(8,128)S(1)}, u32[]{:S(2)}, u32[]{:S(2)}) collective-permute-start(f32[5,64,128]{2,1,0:T(8,128)S(1)} %get-tuple-element.26), channel_id=1, source_target_pairs={{0,4},{4,8},{8,12},{12,0},{1,5},{5,9},{9,13},{13,1},{2,6},{6,10},{... | collective-permute-start | bytes 491528 | tf_op jit(solution)/shard_map/ppermute | solution.py:483
  9.7 13.3 %collective-permute-start.1 = (f32[5,64,128]{2,1,0:T(8,128)S(1)}, f32[5,64,128]{2,1,0:T(8,128)S(1)}, u32[]{:S(2)}, u32[]{:S(2)}) collective-permute-start(f32[5,64,128]{2,1,0:T(8,128)S(1)} %get-tuple-element.27), channel_id=1, source_target_pairs={{0,8},{4,12},{8,0},{12,4},{1,9},{5,13},{9,1},{13,5},{2,10},{6,14},... | collective-permute-start | bytes 491528 | tf_op jit(solution)/shard_map/ppermute | solution.py:483
  12.3 10.7 %collective-permute-start.2 = (f32[5,64,128]{2,1,0:T(8,128)S(1)}, f32[5,64,128]{2,1,0:T(8,128)S(1)}, u32[]{:S(2)}, u32[]{:S(2)}) collective-permute-start(f32[5,64,128]{2,1,0:T(8,128)S(1)} %get-tuple-element.28), channel_id=1, source_target_pairs={{0,12},{4,0},{8,4},{12,8},{1,13},{5,1},{9,5},{13,9},{2,14},{6,2},{... | collective-permute-start | bytes 491528 | tf_op jit(solution)/shard_map/ppermute | solution.py:483
  13.6 16.6 %copy-start.2 = (f32[1280]{0:T(1024)S(1)}, f32[1280]{0:T(1024)}, u32[]{:S(2)}) copy-start(f32[1280]{0:T(1024)} %param.15) | copy-start | bytes 15364
  23.8 8.1 %collective-permute-start.3 = (f32[5,32,128]{2,1,0:T(8,128)S(1)}, f32[5,32,128]{2,1,0:T(8,128)S(1)}, u32[]{:S(2)}, u32[]{:S(2)}) collective-permute-start(f32[5,32,128]{2,1,0:T(8,128)S(1)} %get-tuple-element.40), channel_id=1, source_target_pairs={{0,4},{4,8},{8,12},{12,0},{1,5},{5,9},{9,13},{13,1},{2,6},{6,10},{... | collective-permute-start | bytes 245768 | tf_op jit(solution)/shard_map/ppermute | solution.py:483
  27.8 7.1 %collective-permute-start.4 = (f32[5,32,128]{2,1,0:T(8,128)S(1)}, f32[5,32,128]{2,1,0:T(8,128)S(1)}, u32[]{:S(2)}, u32[]{:S(2)}) collective-permute-start(f32[5,32,128]{2,1,0:T(8,128)S(1)} %get-tuple-element.41), channel_id=1, source_target_pairs={{0,8},{4,12},{8,0},{12,4},{1,9},{5,13},{9,1},{13,5},{2,10},{6,14},... | collective-permute-start | bytes 245768 | tf_op jit(solution)/shard_map/ppermute | solution.py:483
  29.4 6.0 %collective-permute-start.5 = (f32[5,32,128]{2,1,0:T(8,128)S(1)}, f32[5,32,128]{2,1,0:T(8,128)S(1)}, u32[]{:S(2)}, u32[]{:S(2)}) collective-permute-start(f32[5,32,128]{2,1,0:T(8,128)S(1)} %get-tuple-element.42), channel_id=1, source_target_pairs={{0,12},{4,0},{8,4},{12,8},{1,13},{5,1},{9,5},{13,9},{2,14},{6,2},{... | collective-permute-start | bytes 245768 | tf_op jit(solution)/shard_map/ppermute | solution.py:483
